TPU v7x, 256 devices: a whole 4x4x8 slice. The times are simulated.
256 devices in a mesh: dp: 2 (over core), seq: 8 (over z), expert: 16 (over y, x).
Axes of the slice: x: 4, y: 4, z: 8, core: 2. Of those that a mesh axis runs over, the one named last changes fastest.
Arguments:
- tokens: bfloat16 [16384, 2048], P(('dp', 'seq')), may hold values from -6 to 6
- phi: bfloat16 [2048, 32], P(None, 'expert'), may hold values from -40 to 40
- w_in: bfloat16 [32, 2048, 8192], P('expert', None, ('dp', 'seq')), may hold values from -1 to 1
- w_out: bfloat16 [32, 8192, 2048], P('expert', ('dp', 'seq')), may hold values from -0.25 to 0.25
Outputs:
- mixed: bfloat16 [16384, 2048], P(('dp', 'seq', 'expert'))
All inputs are finite; a program needn't handle non-finite values.
Results may differ from a plain program's by a relative error of at most 0.0068.
Values may be sent and summed in bfloat16 or wider, within the bound.
A program may use at most 64 MiB of HBM per device.

v0:
```python
import jax
import jax.numpy as jnp
from jax import lax
from jax.sharding import PartitionSpec as P


def on_device(tokens, phi, w_in, w_out):
    logits = lax.dot_general(
        phi, tokens, (((0,), (1,)), ((), ())), preferred_element_type=jnp.float32
    )
    slot_max = lax.pmax(jnp.max(logits, axis=1), "seq")
    spread = jnp.exp(logits - slot_max[:, None])
    numerator = jnp.dot(spread.astype(jnp.bfloat16), tokens, preferred_element_type=jnp.float32)
    denominator = jnp.sum(spread, axis=1)
    numer_seq, denom_seq = lax.psum((numerator, denominator), "seq")
    own_slots = (numer_seq / denom_seq[:, None]).astype(jnp.bfloat16)
    slot_in = lax.all_gather(own_slots[None], "dp", axis=0, tiled=True)
    hidden = jax.nn.gelu(
        jnp.einsum("ced,edf->cef", slot_in, w_in, preferred_element_type=jnp.float32),
        approximate=True,
    ).astype(jnp.bfloat16)
    partial_value = jnp.einsum("cef,efd->ced", hidden, w_out, preferred_element_type=jnp.float32)
    totals = lax.psum(partial_value, ("dp", "seq"))
    summed = lax.dynamic_index_in_dim(totals, lax.axis_index("dp"), 0, keepdims=False)
    slot_out = summed.astype(jnp.bfloat16)
    row_max = lax.pmax(jnp.max(logits, axis=0), "expert")
    combine_weights = jnp.exp(logits - row_max[None, :])
    local_numer = lax.dot_general(
        combine_weights.astype(jnp.bfloat16),
        slot_out,
        (((0,), (0,)), ((), ())),
        preferred_element_type=jnp.float32,
    )
    mixed_numer, mixed_denom = (
        lax.psum_scatter(local_numer, "expert", scatter_dimension=0, tiled=True),
        lax.psum_scatter(
            jnp.sum(combine_weights, axis=0), "expert", scatter_dimension=0, tiled=True
        ),
    )
    return (mixed_numer / mixed_denom[:, None]).astype(jnp.bfloat16)


def solution(mesh):
    placed = (
        P(("dp", "seq"), None),
        P(None, "expert"),
        P("expert", None, ("dp", "seq")),
        P("expert", ("dp", "seq"), None),
    )
    return jax.shard_map(
        on_device,
        mesh=mesh,
        in_specs=placed,
        out_specs=P(("dp", "seq", "expert"), None),
        check_vma=False,
    )
```

profile of v0, /device:TPU:2, one launch (start us, length us, event | category | flops | bytes accessed | tf_op | source)
XLA Modules:
  0.0 258.3 jit_solution(14364468299653725748)
XLA Ops:
  6.5 0.0 copy-start
  6.5 0.0 reduce-scatter.2.cloned.1.call-start
  6.5 0.7 copy-done
  7.2 3.5 %fusion.35 = (f32[1024]{0:T(1024)S(1)}, f32[2]{0:T(128)S(1)}, f32[2,1024]{1,0:T(2,128)S(1)}) fusion(bf16[2048,2]{0,1:T(2,128)(2,1)S(1)} %copy-done, bf16[1024,2048]{1,0:T(8,128)(2,1)} %param.4), kind=kOutput, calls=%fused_computation.35 | convolution fusion | flops 8391678 | bytes 4214792 | tf_op jit(solution)/shard_map/dot_general | solution.py:8
  10.7 37.7 %pmax.14 = f32[1024]{0:T(1024)S(1)} all-reduce(f32[1024]{0:T(1024)S(1)} %get-tuple-element.7), channel_id=1, replica_groups=mesh['dp'=2,'seq'=8,'expert'=16] {'expert'}, use_global_device_ids=true, to_apply=%region_1.0 | all-reduce | flops 1024 | bytes 8192 | tf_op jit(solution)/shard_map/pmax | solution.py:26
  48.4 19.0 %pmax.15 = f32[2]{0:T(128)S(1)} all-reduce(f32[2]{0:T(128)S(1)} %get-tuple-element.8), channel_id=1, replica_groups=mesh['dp'=2,'seq'=8,'expert'=16] {'seq'}, use_global_device_ids=true, to_apply=%region_3.0 | all-reduce | flops 2 | bytes 16 | tf_op jit(solution)/shard_map/pmax | solution.py:11
  67.4 2.9 %fusion.23 = f32[2,2048]{1,0:T(2,128)S(1)} fusion(bf16[1024,2048]{1,0:T(8,128)(2,1)} %param.4, f32[2,1024]{1,0:T(2,128)S(1)} %get-tuple-element.11, f32[2]{0:T(128)S(1)} %pmax.15), kind=kOutput, calls=%fused_computation.25 | convolution fusion | flops 8392704 | bytes 4218888 | tf_op jit(solution)/shard_map/dot_general | solution.py:13
  70.3 0.2 fusion.19
  70.5 27.1 %all-reduce.1 = (f32[2,2048]{1,0:T(2,128)S(1)}, f32[2]{0:T(128)S(1)}) all-reduce(f32[2,2048]{1,0:T(2,128)S(1)} %fusion.23, f32[2]{0:T(128)S(1)} %get-tuple-element.6), channel_id=1, replica_groups=mesh['dp'=2,'seq'=8,'expert'=16] {'seq'}, use_global_device_ids=true, to_apply=%region_4.0 | all-reduce | flops 4098 | bytes 32784 | tf_op jit(solution)/shard_map/psum | solution.py:15
  97.6 0.1 fusion.18
  97.6 1.8 all-gather.1
  99.4 4.7 %convolution_bitcast_fusion = f32[2,2,2048]{2,0,1:T(2,128)S(1)} fusion(bf16[2,512,2048]{2,1,0:T(8,128)(2,1)} %param.7, bf16[2,2048,512]{2,1,0:T(8,128)(2,1)} %param.6, bf16[2,2,2048]{2,1,0:T(2,128)(2,1)S(1)} %all-gather.1), kind=kOutput, calls=%fused_computation | convolution fusion | flops 16795648 | bytes 8437760 | tf_op jit(solution)/shard_map/cef,efd->ced/dot_general | solution.py:22
  104.1 50.2 %psum.23 = bf16[2,2,2048]{2,0,1:T(2,128)(2,1)S(1)} all-reduce(f32[2,2,2048]{2,0,1:T(2,128)S(1)} %convolution_bitcast_fusion), channel_id=1, replica_groups=mesh['dp'=2,'seq'=8,'expert'=16] {'dp','seq'}, use_global_device_ids=true, to_apply=%region_7.8 | all-reduce | flops 8192 | bytes 49152 | tf_op jit(solution)/shard_map/psum | solution.py:23
  154.3 4.5 %fusion.15 = f32[1024,2048]{1,0:T(8,128)} fusion(bf16[1,2,2048]{2,0,1:T(2,128)(2,1)S(1)} %dynamic-slice_convert_fusion, f32[2,1024]{1,0:T(2,128)S(1)} %get-tuple-element.11, f32[1024]{0:T(1024)S(1)} %pmax.14), kind=kOutput, calls=%fused_computation.15 | convolution fusion | flops 8392704 | bytes 8409088 | tf_op jit(solution)/shard_map/dot_general | solution.py:28
  158.9 0.0 copy-start.1
  158.9 0.0 reduce-scatter.2.cloned.1.call-update
  158.9 0.6 copy-done.1
  159.5 0.6 dynamic-slice
  160.8 40.2 %all-reduce = f32[1024]{0:T(1024)S(1)} all-reduce(f32[1024]{0:T(1024)S(1)} %get-tuple-element.5), channel_id=4, replica_groups=mesh['dp'=2,'seq'=8,'expert'=16] {'expert'}, use_global_device_ids=true, to_apply=%region_10.11.clone | all-reduce | flops 1024 | bytes 8192
  201.0 0.1 dynamic-slice.1
  201.1 48.5 %reduce-scatter.2.cloned.1.call-done = f32[64,2048]{1,0:T(8,128)} async-done(((f32[1024,2048]{1,0:T(8,128)}), f32[64,2048]{1,0:T(8,128)}) %reduce-scatter.2.cloned.1.call-update) | async-done | bytes 524304 | tf_op jit(solution)/shard_map/reduce_scatter | solution.py:35
  249.6 1.8 divide_convert_fusion
  (1 shorter events, 0.0 us)
Async XLA Ops:
  6.5 0.7 copy-start
  6.5 243.0 %reduce-scatter.2.cloned.1.call-start = ((), (), s32[]{:S(2)}) async-start(), calls=%async_computation.1 | async-start | bytes 8912896 | tf_op jit(solution)/shard_map/reduce_scatter | solution.py:35
  158.9 0.7 copy-start.1
Sparse Core Ops, SparseCore 0:
  159.0 90.5 reduce-scatter.1
where the time goes:
time: 259 us; the launch traced here: 258 us
  blocking collectives  176 us (68%)
  waiting for transfers between devices  48.5 us (19%)
  matrix products  15.6 us (6%)
  between operations  14.1 us (5%)
    psum x1, blocking collectives, on_device(): totals = lax.psum(partial_value, ('dp', 'seq'))  50.2 us
    reduce_scatter x1, waiting for transfers between devices, on_device(): lax.psum_scatter(local_numer, 'expert', scatter_dimension=0, tiled=True)  48.5 us
    unnamed x1, blocking collectives  40.2 us
    pmax x1, blocking collectives, on_device(): row_max = lax.pmax(jnp.max(logits, axis=0), 'expert')  37.7 us
    psum x1, blocking collectives, on_device(): numer_seq, denom_seq = lax.psum((numerator, denominator), 'seq')  27.1 us
    pmax x1, blocking collectives, on_device(): slot_max = lax.pmax(jnp.max(logits, axis=1), 'seq')  19 us
  transfers between devices with their start and end apart: 1, of which 1 were waited for; matrix products, arithmetic and copies ran while one was open for 0% of the time, Pallas kernels for 0%

commit v1 on v0

--- a/solution.py
+++ b/solution.py
@@ -5,6 +5,9 @@
 
 
 def on_device(tokens, phi, w_in, w_out):
+    n_expert = lax.axis_size("expert")
+    rows_out = tokens.shape[0] // n_expert
+    phi_all = lax.all_gather(phi, "expert", axis=1, tiled=True)
     logits = lax.dot_general(
         phi, tokens, (((0,), (1,)), ((), ())), preferred_element_type=jnp.float32
     )
@@ -22,21 +25,20 @@
     partial_value = jnp.einsum("cef,efd->ced", hidden, w_out, preferred_element_type=jnp.float32)
     totals = lax.psum(partial_value, ("dp", "seq"))
     summed = lax.dynamic_index_in_dim(totals, lax.axis_index("dp"), 0, keepdims=False)
-    slot_out = summed.astype(jnp.bfloat16)
-    row_max = lax.pmax(jnp.max(logits, axis=0), "expert")
-    combine_weights = jnp.exp(logits - row_max[None, :])
-    local_numer = lax.dot_general(
+    slot_out = lax.all_gather(summed.astype(jnp.bfloat16), "expert", axis=0, tiled=True)
+    rows = lax.dynamic_slice_in_dim(tokens, lax.axis_index("expert") * rows_out, rows_out, 0)
+    row_logits = lax.dot_general(
+        phi_all, rows, (((0,), (1,)), ((), ())), preferred_element_type=jnp.float32
+    )
+    row_max = jnp.max(row_logits, axis=0)
+    combine_weights = jnp.exp(row_logits - row_max[None, :])
+    mixed_numer = lax.dot_general(
         combine_weights.astype(jnp.bfloat16),
         slot_out,
         (((0,), (0,)), ((), ())),
         preferred_element_type=jnp.float32,
     )
-    mixed_numer, mixed_denom = (
-        lax.psum_scatter(local_numer, "expert", scatter_dimension=0, tiled=True),
-        lax.psum_scatter(
-            jnp.sum(combine_weights, axis=0), "expert", scatter_dimension=0, tiled=True
-        ),
-    )
+    mixed_denom = jnp.sum(combine_weights, axis=0)
     return (mixed_numer / mixed_denom[:, None]).astype(jnp.bfloat16)
 
 

time: 259 us -> 160 us (0.62)
  waiting for transfers between devices: 48.5 us -> 0 us
  blocking collectives: 176 us -> 145 us
  between operations: 14.1 us -> 0.03 us
    reduce_scatter x1 -> x0, waiting for transfers between devices: 48.5 us -> none  [on_device(): lax.psum_scatter(local_numer, 'expert', scatter_dimension=0, tiled=True)]
    all_gather x0 -> x2, blocking collectives: none -> 45.8 us  [the longest x1 23.7 us: on_device(): phi_all = lax.all_gather(phi, 'expert', axis=1, tiled=True)]
    unnamed x1 -> x0, blocking collectives: 40.2 us -> none
    pmax x1 -> x0, blocking collectives: 37.7 us -> none  [on_device(): row_max = lax.pmax(jnp.max(logits, axis=0), 'expert')]
    dot_general x1, matrix products: 4.53 us -> 0.98 us  [on_device(): lax.dot_general(combine_weights.astype(jnp.bfloat16), slot_out, (((0,), (...]
  transfers between devices with their start and end apart: 1 -> 0, of which waited for: 1 -> 0; matrix products, arithmetic and copies ran while one was open for 0% -> 0% of each run, Pallas kernels for 0% -> 0%
where the time goes in v1:
time: 160 us; the launch traced here: 158 us
  blocking collectives  145 us (91%)
  matrix products  13.2 us (8%)
    psum x1, blocking collectives, on_device(): totals = lax.psum(partial_value, ('dp', 'seq'))  50.2 us
    psum x1, blocking collectives, on_device(): numer_seq, denom_seq = lax.psum((numerator, denominator), 'seq')  27.1 us
    all_gather x1, blocking collectives, on_device(): phi_all = lax.all_gather(phi, 'expert', axis=1, tiled=True)  23.7 us
    all_gather x1, blocking collectives, on_device(): lax.all_gather(summed.astype(jnp.bfloat16), 'expert', axis=0, tiled=True)  22.1 us
    pmax x1, blocking collectives, on_device(): slot_max = lax.pmax(jnp.max(logits, axis=1), 'seq')  20 us
    dot_general x1, matrix products, on_device(): jnp.einsum('cef,efd->ced', hidden, w_out, preferred_element_type=jnp.floa...  4.66 us
    dot_general x1, matrix products, on_device(): lax.dot_general(phi, tokens, (((0,), (1,)), ((), ())), preferred_element_...  3.5 us

profile of v1, /device:TPU:2, one launch (start us, length us, event | category | flops | bytes accessed | tf_op | source)
XLA Modules:
  0.0 158.5 jit_solution(6288700102996713554)
XLA Ops:
  0.0 3.5 %fusion.39 = (f32[2]{0:T(128)S(1)}, f32[2,1024]{1,0:T(2,128)S(1)}) fusion(bf16[2048,2]{0,1:T(2,128)(2,1)} %param.5, bf16[1024,2048]{1,0:T(8,128)(2,1)} %param.4), kind=kOutput, calls=%fused_computation.39 | convolution fusion | flops 8390654 | bytes 4210696 | tf_op jit(solution)/shard_map/dot_general | solution.py:11
  3.5 20.0 %pmax.7 = f32[2]{0:T(128)S(1)} all-reduce(f32[2]{0:T(128)S(1)} %get-tuple-element.9), channel_id=1, replica_groups=mesh['dp'=2,'seq'=8,'expert'=16] {'seq'}, use_global_device_ids=true, to_apply=%region_2.0 | all-reduce | flops 2 | bytes 16 | tf_op jit(solution)/shard_map/pmax | solution.py:14
  23.5 0.2 fusion.25
  23.7 2.9 %fusion.27 = f32[2,2048]{1,0:T(2,128)S(1)} fusion(bf16[1024,2048]{1,0:T(8,128)(2,1)} %param.4, f32[2,1024]{1,0:T(2,128)S(1)} %get-tuple-element.10, f32[2]{0:T(128)S(1)} %pmax.7), kind=kOutput, calls=%fused_computation.28 | convolution fusion | flops 8392704 | bytes 4218888 | tf_op jit(solution)/shard_map/dot_general | solution.py:16
  26.6 27.1 %all-reduce = (f32[2,2048]{1,0:T(2,128)S(1)}, f32[2]{0:T(128)S(1)}) all-reduce(f32[2,2048]{1,0:T(2,128)S(1)} %fusion.27, f32[2]{0:T(128)S(1)} %fusion.25), channel_id=1, replica_groups=mesh['dp'=2,'seq'=8,'expert'=16] {'seq'}, use_global_device_ids=true, to_apply=%region_3.0 | all-reduce | flops 4098 | bytes 32784 | tf_op jit(solution)/shard_map/psum | solution.py:18
  53.7 0.1 fusion.24
  53.7 1.8 %all-gather.3 = bf16[2,2,2048]{2,1,0:T(2,128)(2,1)S(1)} all-gather(bf16[1,2,2048]{2,1,0:T(2,128)(2,1)S(1)} %fusion.24), channel_id=2, replica_groups=mesh['dp'=2,'seq'=8,'expert'=16] {'dp'}, dimensions={0}, use_global_device_ids=true | all-gather | bytes 24576 | tf_op jit(solution)/shard_map/all_gather | solution.py:20
  55.5 0.0 copy-start
  55.5 4.7 %convolution_bitcast_fusion = f32[2,2,2048]{2,0,1:T(2,128)S(1)} fusion(bf16[2,512,2048]{2,1,0:T(8,128)(2,1)} %param.7, bf16[2,2048,512]{2,1,0:T(8,128)(2,1)} %param.6, bf16[2,2,2048]{2,1,0:T(2,128)(2,1)S(1)} %all-gather.3), kind=kOutput, calls=%fused_computation.2 | convolution fusion | flops 16795648 | bytes 8437760 | tf_op jit(solution)/shard_map/cef,efd->ced/dot_general | solution.py:25
  60.2 50.2 %psum.23 = bf16[2,2,2048]{2,0,1:T(2,128)(2,1)S(1)} all-reduce(f32[2,2,2048]{2,0,1:T(2,128)S(1)} %convolution_bitcast_fusion), channel_id=1, replica_groups=mesh['dp'=2,'seq'=8,'expert'=16] {'dp','seq'}, use_global_device_ids=true, to_apply=%region_6.7 | all-reduce | flops 8192 | bytes 49152 | tf_op jit(solution)/shard_map/psum | solution.py:26
  110.4 0.0 copy-done
  110.5 23.7 %all-gather.2 = bf16[16,2,2048]{2,1,0:T(2,128)(2,1)S(1)} all-gather(bf16[1,2,2048]{2,1,0:T(2,128)(2,1)S(1)} %bitcast.24), channel_id=1, replica_groups=mesh['dp'=2,'seq'=8,'expert'=16] {'expert'}, dimensions={0}, use_global_device_ids=true | all-gather | bytes 139264 | tf_op jit(solution)/shard_map/all_gather | solution.py:10
  134.1 0.1 reshape.8
  134.2 1.2 fusion.38
  135.4 22.1 %all-gather.1 = bf16[1,32,2048]{2,0,1:T(2,128)(2,1)S(1)} all-gather(bf16[1,2,2048]{2,0,1:T(2,128)(2,1)S(1)} %dynamic-slice_convert_fusion), channel_id=3, replica_groups=mesh['dp'=2,'seq'=8,'expert'=16] {'expert'}, dimensions={1}, use_global_device_ids=true | all-gather | bytes 139264 | tf_op jit(solution)/shard_map/all_gather | solution.py:28
  157.5 1.0 fusion
  (2 shorter events, 0.1 us)
Async XLA Ops:
  55.5 54.9 %copy-start = (bf16[2048,2]{0,1:T(2,128)(2,1)S(1)}, bf16[2048,2]{0,1:T(2,128)(2,1)}, u32[]{:S(2)}) copy-start(bf16[2048,2]{0,1:T(2,128)(2,1)} %param.5) | copy-start | bytes 24580

commit v2 on v1

v2 whole, which is shorter than its diff:
```python
import functools

import jax
import jax.numpy as jnp
from jax import lax
from jax.experimental import pallas as pl
from jax.experimental.pallas import tpu as pltpu
from jax.sharding import PartitionSpec as P

MESH = pl.DeviceIdType.MESH
AXES = ("dp", "seq", "expert")


def _peer_coords(group, rank):
    coords = {a: lax.axis_index(a) for a in AXES}
    sizes = [lax.axis_size(a) for a in group]
    rest = rank
    for a, s in reversed(list(zip(group, sizes))):
        coords[a] = lax.rem(rest, s)
        rest = rest // s
    return tuple(coords[a] for a in AXES)


def _my_rank(group):
    rank = 0
    for a in group:
        rank = rank * lax.axis_size(a) + lax.axis_index(a)
    return rank


def _exchange_kernel(group, n, select, x_ref, o_ref, land, send_sem, recv_sem):
    me = _my_rank(group)
    barrier = pltpu.get_barrier_semaphore()
    for k in range(1, n):
        peer = _peer_coords(group, lax.rem(me + k, n))
        pl.semaphore_signal(barrier, inc=1, device_id=peer, device_id_type=MESH)
    pl.semaphore_wait(barrier, n - 1)

    def src_for(coords):
        if select is None:
            return x_ref
        return x_ref.at[coords[AXES.index(select)]]

    copies = []
    for k in range(1, n):
        peer = _peer_coords(group, lax.rem(me + k, n))
        copy = pltpu.make_async_remote_copy(
            src_ref=src_for(peer),
            dst_ref=land.at[me],
            send_sem=send_sem.at[k],
            recv_sem=recv_sem.at[k],
            device_id=peer,
            device_id_type=MESH,
        )
        copy.start()
        copies.append(copy)
    for copy in copies:
        copy.wait_send()
    for k in range(1, n):
        src_rank = lax.rem(me + n - k, n)
        pltpu.make_async_remote_copy(
            src_ref=src_for(_peer_coords(group, src_rank)),
            dst_ref=land.at[src_rank],
            send_sem=send_sem.at[k],
            recv_sem=recv_sem.at[k],
            device_id=_peer_coords(group, src_rank),
            device_id_type=MESH,
        ).wait_recv()
    o_ref[...] = land[...]
    own = src_for(_peer_coords(group, me))
    o_ref[me] = own[...]


def exchange(x, group, cid, select=None):
    n = 1
    for a in group:
        n *= lax.axis_size(a)
    block = x.shape if select is None else x.shape[1:]
    return pl.pallas_call(
        functools.partial(_exchange_kernel, group, n, select),
        out_shape=jax.ShapeDtypeStruct((n,) + block, x.dtype),
        in_specs=[pl.BlockSpec(memory_space=pltpu.VMEM)],
        out_specs=pl.BlockSpec(memory_space=pltpu.VMEM),
        scratch_shapes=[
            pltpu.VMEM((n,) + block, x.dtype),
            pltpu.SemaphoreType.DMA((n,)),
            pltpu.SemaphoreType.DMA((n,)),
        ],
        compiler_params=pltpu.CompilerParams(collective_id=cid, has_side_effects=True),
    )(x)


def on_device(tokens, phi, w_in, w_out):
    n_expert = lax.axis_size("expert")
    n_dp = lax.axis_size("dp")
    n_seq = lax.axis_size("seq")
    own_e = phi.shape[1]
    d = tokens.shape[1]
    rows_out = tokens.shape[0] // n_expert
    logits = lax.dot_general(
        phi, tokens, (((0,), (1,)), ((), ())), preferred_element_type=jnp.float32
    )
    local_max = jnp.broadcast_to(jnp.max(logits, axis=1)[:, None], (own_e, 128))
    slot_max = jnp.max(exchange(local_max, ("seq",), 0), axis=0)[:, 0]
    spread = jnp.exp(logits - slot_max[:, None])
    numerator = jnp.dot(spread.astype(jnp.bfloat16), tokens, preferred_element_type=jnp.float32)
    denominator = jnp.broadcast_to(jnp.sum(spread, axis=1)[:, None], (own_e, 128))
    stats = exchange(jnp.concatenate([numerator, denominator], axis=1), ("dp", "seq"), 1)
    stats = jnp.sum(stats.reshape(n_dp, n_seq, own_e, d + 128), axis=1)
    slot_in = (stats[:, :, :d] / stats[:, :, d:d + 1]).astype(jnp.bfloat16)
    hidden = jax.nn.gelu(
        jnp.einsum("ced,edf->cef", slot_in, w_in, preferred_element_type=jnp.float32),
        approximate=True,
    ).astype(jnp.bfloat16)
    partial_value = jnp.einsum("cef,efd->ced", hidden, w_out, preferred_element_type=jnp.float32)
    summed = jnp.sum(exchange(partial_value, ("dp", "seq"), 2, select="dp"), axis=0)
    packed = jnp.concatenate([phi.T, summed.astype(jnp.bfloat16)], axis=0)
    gathered = exchange(packed, ("expert",), 3)
    phi_all = gathered[:, :own_e].reshape(n_expert * own_e, d)
    slot_out = gathered[:, own_e:].reshape(n_expert * own_e, d)
    rows = lax.dynamic_slice_in_dim(tokens, lax.axis_index("expert") * rows_out, rows_out, 0)
    row_logits = lax.dot_general(
        phi_all, rows, (((1,), (1,)), ((), ())), preferred_element_type=jnp.float32
    )
    row_max = jnp.max(row_logits, axis=0)
    combine_weights = jnp.exp(row_logits - row_max[None, :])
    mixed_numer = lax.dot_general(
        combine_weights.astype(jnp.bfloat16),
        slot_out,
        (((0,), (0,)), ((), ())),
        preferred_element_type=jnp.float32,
    )
    mixed_denom = jnp.sum(combine_weights, axis=0)
    return (mixed_numer / mixed_denom[:, None]).astype(jnp.bfloat16)


def solution(mesh):
    placed = (
        P(("dp", "seq"), None),
        P(None, "expert"),
        P("expert", None, ("dp", "seq")),
        P("expert", ("dp", "seq"), None),
    )
    return jax.shard_map(
        on_device,
        mesh=mesh,
        in_specs=placed,
        out_specs=P(("dp", "seq", "expert"), None),
        check_vma=False,
    )
```

time: 160 us -> 71.9 us (0.45)
  blocking collectives: 145 us -> 0 us
  Pallas kernels: 0 us -> 50.5 us
  other arithmetic: 0.31 us -> 4.36 us
  local copies, waits for them, and re-layouts: 0.08 us -> 2.97 us
    psum x2 -> x0, blocking collectives: 77.3 us -> none  [the longest x1 50.2 us: on_device(): totals = lax.psum(partial_value, ('dp', 'seq'))]
    pallas_call x0 -> x4, Pallas kernels: none -> 50.5 us  [exchange(): pl.pallas_call(functools.partial(_exchange_kernel, group, n, select), out...]
    all_gather x3 -> x0, blocking collectives: 47.6 us -> none  [the longest x1 23.7 us: on_device(): phi_all = lax.all_gather(phi, 'expert', axis=1, tiled=True)]
    pmax x1 -> x0, blocking collectives: 20 us -> none  [on_device(): slot_max = lax.pmax(jnp.max(logits, axis=1), 'seq')]
    reduce_sum x1 -> x3, other arithmetic: 0.2 us -> 2.28 us  [the longest x1 1.04 us: on_device(): jnp.sum(exchange(partial_value, ('dp', 'seq'), 2, select='dp'), axis=0)]
where the time goes in v2:
time: 71.9 us; the launch traced here: 71.1 us
  Pallas kernels  50.5 us (70%)
  matrix products  13.2 us (18%)
  other arithmetic  4.36 us (6%)
  local copies, waits for them, and re-layouts  2.97 us (4%)
    pallas_call x4, Pallas kernels, exchange(): pl.pallas_call(functools.partial(_exchange_kernel, group, n, select), out...  50.5 us
    dot_general x1, matrix products, on_device(): jnp.einsum('cef,efd->ced', hidden, w_out, preferred_element_type=jnp.floa...  4.66 us
    dot_general x1, matrix products, on_device(): lax.dot_general(phi, tokens, (((0,), (1,)), ((), ())), preferred_element_...  3.5 us
    dot_general x1, matrix products, on_device(): jnp.dot(spread.astype(jnp.bfloat16), tokens, preferred_element_type=jnp.f...  2.88 us

profile of v2, /device:TPU:2, one launch (start us, length us, event | category | flops | bytes accessed | tf_op | source)
XLA Modules:
  0.0 71.1 jit_solution(18253429082743393305)
XLA Ops:
  0.0 3.5 %fusion.38 = (f32[2]{0:T(128)S(1)}, f32[2,1024]{1,0:T(2,128)S(1)}) fusion(bf16[2048,2]{0,1:T(2,128)(2,1)} %param.5, bf16[1024,2048]{1,0:T(8,128)(2,1)} %param.4), kind=kOutput, calls=%fused_computation.42 | convolution fusion | flops 8390654 | bytes 4210696 | tf_op jit(solution)/shard_map/dot_general | solution.py:100
  3.5 0.6 broadcast_in_dim.4.x_ref
  4.1 12.1 %shard_map.46 = f32[8,2,128]{2,1,0:T(2,128)} custom-call(f32[2,128]{1,0:T(2,128)} %broadcast_in_dim.4.x_ref), custom_call_target="tpu_custom_call" | custom-call | tf_op jit(solution)/shard_map/pallas_call | solution.py:79
  16.3 0.7 %reduce_max.28 = f32[2,128]{1,0:T(2,128)S(1)} reduce(f32[8,2,128]{2,1,0:T(2,128)} %shard_map.46, f32[]{:T(128)} %constant.10.clone.1), dimensions={0}, to_apply=%region_1.0 | reduce | flops 1792 | bytes 9220 | tf_op jit(solution)/shard_map/reduce_max | solution.py:104
  17.0 0.1 slice_reduce_fusion.1
  17.1 2.9 %fusion.26 = f32[2,2048]{1,0:T(2,128)S(1)} fusion(bf16[1024,2048]{1,0:T(8,128)(2,1)} %param.4, f32[2,1024]{1,0:T(2,128)S(1)} %get-tuple-element.8, f32[2]{0:T(128)S(1)} %slice_reduce_fusion.1), kind=kOutput, calls=%fused_computation.29 | convolution fusion | flops 8392704 | bytes 4218888 | tf_op jit(solution)/shard_map/dot_general | solution.py:106
  20.0 0.2 fusion.24
  20.2 0.1 broadcast_in_dim.5
  20.3 0.6 pad_maximum_fusion.x_ref
  20.9 13.8 %shard_map.47 = f32[16,2,2176]{2,1,0:T(2,128)} custom-call(f32[2,2176]{1,0:T(2,128)} %pad_maximum_fusion.x_ref), custom_call_target="tpu_custom_call" | custom-call | tf_op jit(solution)/shard_map/pallas_call | solution.py:79
  34.7 1.0 %bitcast_reduce_fusion = f32[2,2,2176]{2,1,0:T(2,128)S(1)} fusion(f32[16,2,2176]{2,1,0:T(2,128)} %shard_map.47), kind=kLoop, calls=%fused_computation.3 | loop fusion | flops 60928 | bytes 313344 | tf_op jit(solution)/shard_map/reduce_sum | solution.py:109
  35.7 0.1 slice_reduce_fusion
  35.8 0.1 fusion.3
  35.9 0.0 copy-start
  35.9 4.7 %fusion.20 = f32[2,2,2048]{2,1,0:T(2,128)S(1)} fusion(bf16[2,512,2048]{2,1,0:T(8,128)(2,1)} %param.7, bf16[2,2048,512]{2,1,0:T(8,128)(2,1)} %param.6, bf16[2,2,2048]{2,1,0:T(2,128)(2,1)S(1)} %fusion.3), kind=kOutput, calls=%fused_computation.24 | convolution fusion | flops 16795648 | bytes 8437760 | tf_op jit(solution)/shard_map/cef,efd->ced/dot_general | solution.py:115
  40.6 0.6 copy.20
  41.2 13.5 %shard_map.48 = f32[16,2,2048]{2,1,0:T(2,128)} custom-call(f32[2,2,2048]{2,1,0:T(2,128)} %bitcast.21), custom_call_target="tpu_custom_call" | custom-call | tf_op jit(solution)/shard_map/pallas_call | solution.py:79
  54.7 1.0 %reduce_sum.38 = bf16[2,2048]{1,0:T(2,128)(2,1)S(1)} reduce(f32[16,2,2048]{2,1,0:T(2,128)} %shard_map.48, f32[]{:T(128)} %constant.1.clone.1), dimensions={0}, to_apply=%region_4.0 | reduce | flops 61440 | bytes 270340 | tf_op jit(solution)/shard_map/reduce_sum | solution.py:116
  55.8 0.0 copy-done
  55.8 0.6 pad_maximum_fusion.1.x_ref
  56.4 11.2 %shard_map.49 = bf16[16,4,2048]{2,1,0:T(4,128)(2,1)} custom-call(bf16[4,2048]{1,0:T(4,128)(2,1)} %pad_maximum_fusion.1.x_ref), custom_call_target="tpu_custom_call" | custom-call | tf_op jit(solution)/shard_map/pallas_call | solution.py:79
  67.6 1.3 %fusion.37 = (bf16[16,2,2048]{2,1,0:T(2,128)(2,1)S(1)}, bf16[16,2,2048]{2,1,0:T(2,128)(2,1)S(1)}) fusion(bf16[16,4,2048]{2,1,0:T(4,128)(2,1)} %shard_map.49), kind=kLoop, calls=%fused_computation.41 | loop fusion | bytes 524288 | tf_op jit(solution)/shard_map/slice | solution.py:119
  68.9 0.1 reshape.14
  68.9 1.2 %fusion.39 = (f32[64]{0:T(128)S(1)}, f32[32,64]{1,0:T(8,128)S(1)}) fusion(bf16[32,2048]{1,0:T(8,128)(2,1)S(1)} %reshape.14, bf16[1024,2048]{1,0:T(8,128)(2,1)} %param.4, s32[]{:T(128)S(6)} %select_n.3), kind=kOutput, calls=%fused_computation.43 | convolution fusion | flops 8390592 | bytes 401668 | tf_op jit(solution)/shard_map/dot_general | solution.py:122
  70.1 0.1 reshape.15
  70.2 1.0 %fusion = bf16[64,2048]{1,0:T(8,128)(2,1)} fusion(bf16[32,2048]{1,0:T(8,128)(2,1)S(1)} %reshape.15, f32[64]{0:T(128)S(1)} %fusion.5, f32[32,64]{1,0:T(8,128)S(1)} %get-tuple-element.10, f32[64]{0:T(128)S(1)} %get-tuple-element.9), kind=kOutput, calls=%fused_computation.1 | convolution fusion | flops 8654848 | bytes 401920 | tf_op jit(solution)/shard_map/dot_general | solution.py:127
  (1 shorter events, 0.0 us)
Async XLA Ops:
  35.9 19.8 %copy-start = (bf16[2048,2]{0,1:T(2,128)(2,1)S(1)}, bf16[2048,2]{0,1:T(2,128)(2,1)}, u32[]{:S(2)}) copy-start(bf16[2048,2]{0,1:T(2,128)(2,1)} %param.5) | copy-start | bytes 24580

commit v3 on v2

--- a/solution.py
+++ b/solution.py
@@ -90,6 +90,69 @@
     )(x)
 
 
+def _reduce_then_gather_kernel(g1, n1, g2, n2, x_ref, phi_ref, o_ref, land1, send2, land2, s1, r1, s2, r2):
+    me1, me2 = _my_rank(g1), _my_rank(g2)
+    barrier = pltpu.get_barrier_semaphore()
+    for group, me, n in ((g1, me1, n1), (g2, me2, n2)):
+        for k in range(1, n):
+            peer = _peer_coords(group, lax.rem(me + k, n))
+            pl.semaphore_signal(barrier, inc=1, device_id=peer, device_id_type=MESH)
+    pl.semaphore_wait(barrier, n1 - 1 + n2 - 1)
+
+    def run(group, me, n, src_for, land, ssem, rsem):
+        copies = []
+        for k in range(1, n):
+            peer = _peer_coords(group, lax.rem(me + k, n))
+            copy = pltpu.make_async_remote_copy(
+                src_ref=src_for(peer), dst_ref=land.at[me], send_sem=ssem.at[k],
+                recv_sem=rsem.at[k], device_id=peer, device_id_type=MESH,
+            )
+            copy.start()
+            copies.append(copy)
+        for copy in copies:
+            copy.wait_send()
+        for k in range(1, n):
+            src_rank = lax.rem(me + n - k, n)
+            peer = _peer_coords(group, src_rank)
+            pltpu.make_async_remote_copy(
+                src_ref=src_for(peer), dst_ref=land.at[src_rank], send_sem=ssem.at[k],
+                recv_sem=rsem.at[k], device_id=peer, device_id_type=MESH,
+            ).wait_recv()
+
+    dp_pos = AXES.index("dp")
+    run(g1, me1, n1, lambda c: x_ref.at[c[dp_pos]], land1, s1, r1)
+    land1[me1] = x_ref[lax.axis_index("dp")]
+    total = jnp.sum(land1[...], axis=0)
+    send2[...] = jnp.concatenate([phi_ref[...], total.astype(send2.dtype)], axis=0)
+    run(g2, me2, n2, lambda c: send2, land2, s2, r2)
+    land2[me2] = send2[...]
+    o_ref[...] = land2[...]
+
+
+def reduce_then_gather(x, phi_t, cid):
+    g1, g2 = ("dp", "seq"), ("expert",)
+    n1 = lax.axis_size("dp") * lax.axis_size("seq")
+    n2 = lax.axis_size("expert")
+    rows, d = x.shape[1], x.shape[2]
+    packed = (phi_t.shape[0] + rows, d)
+    return pl.pallas_call(
+        functools.partial(_reduce_then_gather_kernel, g1, n1, g2, n2),
+        out_shape=jax.ShapeDtypeStruct((n2,) + packed, phi_t.dtype),
+        in_specs=[pl.BlockSpec(memory_space=pltpu.VMEM)] * 2,
+        out_specs=pl.BlockSpec(memory_space=pltpu.VMEM),
+        scratch_shapes=[
+            pltpu.VMEM((n1, rows, d), x.dtype),
+            pltpu.VMEM(packed, phi_t.dtype),
+            pltpu.VMEM((n2,) + packed, phi_t.dtype),
+            pltpu.SemaphoreType.DMA((n1,)),
+            pltpu.SemaphoreType.DMA((n1,)),
+            pltpu.SemaphoreType.DMA((n2,)),
+            pltpu.SemaphoreType.DMA((n2,)),
+        ],
+        compiler_params=pltpu.CompilerParams(collective_id=cid, has_side_effects=True),
+    )(x, phi_t)
+
+
 def on_device(tokens, phi, w_in, w_out):
     n_expert = lax.axis_size("expert")
     n_dp = lax.axis_size("dp")
@@ -100,22 +163,26 @@
     logits = lax.dot_general(
         phi, tokens, (((0,), (1,)), ((), ())), preferred_element_type=jnp.float32
     )
-    local_max = jnp.broadcast_to(jnp.max(logits, axis=1)[:, None], (own_e, 128))
-    slot_max = jnp.max(exchange(local_max, ("seq",), 0), axis=0)[:, 0]
-    spread = jnp.exp(logits - slot_max[:, None])
+    local_max = jnp.max(logits, axis=1)
+    spread = jnp.exp(logits - local_max[:, None])
     numerator = jnp.dot(spread.astype(jnp.bfloat16), tokens, preferred_element_type=jnp.float32)
-    denominator = jnp.broadcast_to(jnp.sum(spread, axis=1)[:, None], (own_e, 128))
-    stats = exchange(jnp.concatenate([numerator, denominator], axis=1), ("dp", "seq"), 1)
-    stats = jnp.sum(stats.reshape(n_dp, n_seq, own_e, d + 128), axis=1)
-    slot_in = (stats[:, :, :d] / stats[:, :, d:d + 1]).astype(jnp.bfloat16)
+    denominator = jnp.sum(spread, axis=1)
+    side = jnp.concatenate(
+        [jnp.broadcast_to(denominator[:, None], (own_e, 128)),
+         jnp.broadcast_to(local_max[:, None], (own_e, 128))], axis=1)
+    stats = exchange(jnp.concatenate([numerator, side], axis=1), ("dp", "seq"), 1)
+    stats = stats.reshape(n_dp, n_seq, own_e, d + 256)
+    part_max = stats[:, :, :, d + 128]
+    rescale = jnp.exp(part_max - jnp.max(part_max, axis=1, keepdims=True))
+    numer = jnp.sum(stats[:, :, :, :d] * rescale[..., None], axis=1)
+    denom = jnp.sum(stats[:, :, :, d] * rescale, axis=1)
+    slot_in = (numer / denom[..., None]).astype(jnp.bfloat16)
     hidden = jax.nn.gelu(
         jnp.einsum("ced,edf->cef", slot_in, w_in, preferred_element_type=jnp.float32),
         approximate=True,
     ).astype(jnp.bfloat16)
     partial_value = jnp.einsum("cef,efd->ced", hidden, w_out, preferred_element_type=jnp.float32)
-    summed = jnp.sum(exchange(partial_value, ("dp", "seq"), 2, select="dp"), axis=0)
-    packed = jnp.concatenate([phi.T, summed.astype(jnp.bfloat16)], axis=0)
-    gathered = exchange(packed, ("expert",), 3)
+    gathered = reduce_then_gather(partial_value, phi.T, 2)
     phi_all = gathered[:, :own_e].reshape(n_expert * own_e, d)
     slot_out = gathered[:, own_e:].reshape(n_expert * own_e, d)
     rows = lax.dynamic_slice_in_dim(tokens, lax.axis_index("expert") * rows_out, rows_out, 0)

time: 71.9 us -> 56.4 us (0.78)
  Pallas kernels: 50.5 us -> 38.9 us
  matrix products: 13.2 us -> 11.1 us
  other arithmetic: 4.36 us -> 3.16 us
    pallas_call x4 -> x1, Pallas kernels: 50.5 us -> 17.3 us  [exchange(): pl.pallas_call(functools.partial(_exchange_kernel, group, n, select), out...]
    pallas_call x0 -> x1, Pallas kernels: none -> 21.6 us  [reduce_then_gather(): pl.pallas_call(functools.partial(_reduce_then_gather_kernel, g1, n1, g2,...]
    dot_general x1, matrix products: 2.88 us -> 0.69 us  [on_device(): jnp.dot(spread.astype(jnp.bfloat16), tokens, preferred_element_type=jnp.f...]
    slice x0 -> x1, other arithmetic: none -> 0.83 us  [on_device(): denom = jnp.sum(stats[:, :, :, d] * rescale, axis=1)]
    reduce_sum x3, other arithmetic: 2.28 us -> 1.51 us  [the longest x1 1.15 us: on_device(): numer = jnp.sum(stats[:, :, :, :d] * rescale[..., None], axis=1)]
where the time goes in v3:
time: 56.4 us; the launch traced here: 55.8 us
  Pallas kernels  38.9 us (69%)
  matrix products  11.1 us (20%)
  other arithmetic  3.16 us (6%)
  local copies, waits for them, and re-layouts  2.49 us (4%)
    pallas_call x1, Pallas kernels, reduce_then_gather(): pl.pallas_call(functools.partial(_reduce_then_gather_kernel, g1, n1, g2,...  21.6 us
    pallas_call x1, Pallas kernels, exchange(): pl.pallas_call(functools.partial(_exchange_kernel, group, n, select), out...  17.3 us
    dot_general x1, matrix products, on_device(): jnp.einsum('cef,efd->ced', hidden, w_out, preferred_element_type=jnp.floa...  4.66 us
    dot_general x1, matrix products, on_device(): lax.dot_general(phi, tokens, (((0,), (1,)), ((), ())), preferred_element_...  3.65 us
    slice x1, local copies, waits for them, and re-layouts, on_device(): phi_all = gathered[:, :own_e].reshape(n_expert * own_e, d)  1.29 us
    dot_general x1, matrix products, on_device(): lax.dot_general(phi_all, rows, (((1,), (1,)), ((), ())), preferred_elemen...  1.17 us
    reduce_sum x1, other arithmetic, on_device(): numer = jnp.sum(stats[:, :, :, :d] * rescale[..., None], axis=1)  1.15 us

profile of v3, /device:TPU:2, one launch (start us, length us, event | category | flops | bytes accessed | tf_op | source)
XLA Modules:
  0.0 55.8 jit_solution(10812369086790492054)
XLA Ops:
  0.0 0.0 copy-start
  0.0 3.7 %fusion.42 = (f32[2]{0:T(128)S(1)}, f32[2,1024]{1,0:T(2,128)S(1)}) fusion(bf16[2048,2]{0,1:T(2,128)(2,1)} %param.5, bf16[1024,2048]{1,0:T(8,128)(2,1)} %param.4), kind=kOutput, calls=%fused_computation.46 | convolution fusion | flops 8390654 | bytes 4210696 | tf_op jit(solution)/shard_map/dot_general | solution.py:163
  3.7 0.0 copy-done
  3.7 0.7 %fusion.26 = f32[2,2048]{1,0:T(2,128)S(1)} fusion(bf16[1024,2048]{1,0:T(8,128)(2,1)S(1)} %copy-done, f32[2,1024]{1,0:T(2,128)S(1)} %get-tuple-element.11, f32[2]{0:T(128)S(1)} %get-tuple-element.10), kind=kOutput, calls=%fused_computation.28 | convolution fusion | flops 8392704 | bytes 4218888 | tf_op jit(solution)/shard_map/dot_general | solution.py:168
  4.4 0.2 fusion.24
  4.6 0.1 broadcast_in_dim.4
  4.6 0.1 broadcast_in_dim.5
  4.7 0.6 %pad_maximum_fusion.x_ref = f32[2,2304]{1,0:T(2,128)} fusion(f32[2,128]{1,0:T(2,128)S(1)} %broadcast_in_dim.5, f32[2,128]{1,0:T(2,128)S(1)} %broadcast_in_dim.4, f32[2,2048]{1,0:T(2,128)S(1)} %fusion.26), kind=kLoop, calls=%fused_computation.9 | loop fusion | flops 9216 | bytes 36864 | tf_op jit(solution)/shard_map/concatenate | solution.py:173
  5.3 17.3 %shard_map.46 = f32[16,2,2304]{2,1,0:T(2,128)} custom-call(f32[2,2304]{1,0:T(2,128)} %pad_maximum_fusion.x_ref), custom_call_target="tpu_custom_call" | custom-call | tf_op jit(solution)/shard_map/pallas_call | solution.py:79
  22.7 0.8 %fusion.40 = (f32[2,8,2,1]{3,2,1,0:T(2,128)S(1)}, f32[2,2]{1,0:T(2,128)S(1)}, f32[2,8,2,1]{3,2,1,0:T(2,128)S(1)}) fusion(f32[2,8,2,2304]{3,2,1,0:T(2,128)} %bitcast.32), kind=kLoop, calls=%fused_computation.44 | loop fusion | flops 28 | bytes 528 | tf_op jit(solution)/shard_map/slice | solution.py:178
  23.5 0.1 copy.14
  23.6 0.1 copy.15
  23.7 0.2 fusion.34
  23.9 0.1 exponential_bitcast_fusion
  23.9 0.1 copy.10
  24.0 1.2 %fusion.1 = f32[2,2,2048]{2,1,0:T(2,128)S(1)} fusion(f32[2,8,2,2304]{3,2,1,0:T(2,128)} %bitcast.33, f32[2,8,2]{2,1,0:T(8,128)S(1)} %copy.10), kind=kLoop, calls=%fused_computation.4 | loop fusion | flops 122880 | bytes 295040 | tf_op jit(solution)/shard_map/reduce_sum | solution.py:177
  25.2 0.1 divide_convert_fusion
  25.3 4.7 %fusion.20 = f32[2,2,2048]{2,1,0:T(2,128)S(1)} fusion(bf16[2,512,2048]{2,1,0:T(8,128)(2,1)} %param.7, bf16[2,2048,512]{2,1,0:T(8,128)(2,1)} %param.6, bf16[2,2,2048]{2,1,0:T(2,128)(2,1)S(1)} %divide_convert_fusion), kind=kOutput, calls=%fused_computation.23 | convolution fusion | flops 16795648 | bytes 8437760 | tf_op jit(solution)/shard_map/cef,efd->ced/dot_general | solution.py:184
  29.9 0.6 %copy.26 = f32[2,2,2048]{2,0,1:T(2,128)} copy(f32[2,2,2048]{2,1,0:T(2,128)S(1)} %fusion.20) | data formatting | bytes 65536 | tf_op jit(solution)/shard_map/cef,efd->ced/dot_general | solution.py:184
  30.6 21.6 %shard_map.47 = bf16[16,4,2048]{2,1,0:T(4,128)(2,1)} custom-call(f32[2,2,2048]{2,1,0:T(2,128)} %bitcast.34, bf16[2,2048]{1,0:T(2,128)(2,1)} %bitcast.35), custom_call_target="tpu_custom_call" | custom-call | tf_op jit(solution)/shard_map/pallas_call | solution.py:138
  52.2 1.3 %fusion.41 = (bf16[16,2,2048]{2,1,0:T(2,128)(2,1)S(1)}, bf16[16,2,2048]{2,1,0:T(2,128)(2,1)S(1)}) fusion(bf16[16,4,2048]{2,1,0:T(4,128)(2,1)} %shard_map.47), kind=kLoop, calls=%fused_computation.45 | loop fusion | bytes 524288 | tf_op jit(solution)/shard_map/slice | solution.py:186
  53.5 0.1 reshape.16
  53.5 1.2 %fusion.43 = (f32[64]{0:T(128)S(1)}, f32[32,64]{1,0:T(8,128)S(1)}) fusion(bf16[32,2048]{1,0:T(8,128)(2,1)S(1)} %reshape.16, bf16[1024,2048]{1,0:T(8,128)(2,1)} %param.4, s32[]{:T(128)S(6)} %select_n.3), kind=kOutput, calls=%fused_computation.47 | convolution fusion | flops 8390592 | bytes 401668 | tf_op jit(solution)/shard_map/dot_general | solution.py:189
  54.7 0.1 reshape.17
  54.8 1.0 %fusion = bf16[64,2048]{1,0:T(8,128)(2,1)} fusion(bf16[32,2048]{1,0:T(8,128)(2,1)S(1)} %reshape.17, f32[64]{0:T(128)S(1)} %fusion.5, f32[32,64]{1,0:T(8,128)S(1)} %get-tuple-element.13, f32[64]{0:T(128)S(1)} %get-tuple-element.12), kind=kOutput, calls=%fused_computation.1 | convolution fusion | flops 8654848 | bytes 401920 | tf_op jit(solution)/shard_map/dot_general | solution.py:194
  (1 shorter events, 0.0 us)
Async XLA Ops:
  0.0 3.7 %copy-start = (bf16[1024,2048]{1,0:T(8,128)(2,1)S(1)}, bf16[1024,2048]{1,0:T(8,128)(2,1)}, u32[]{:S(2)}) copy-start(bf16[1024,2048]{1,0:T(8,128)(2,1)} %param.4) | copy-start | bytes 12582916

commit v4 on v2

--- a/solution.py
+++ b/solution.py
@@ -90,6 +90,131 @@
     )(x)
 
 
+def _send_all(group, me, n, src_for, land, ssem, rsem):
+    copies = []
+    for k in range(1, n):
+        peer = _peer_coords(group, lax.rem(me + k, n))
+        copy = pltpu.make_async_remote_copy(
+            src_ref=src_for(peer), dst_ref=land.at[me], send_sem=ssem.at[k],
+            recv_sem=rsem.at[k], device_id=peer, device_id_type=MESH,
+        )
+        copy.start()
+        copies.append(copy)
+    return copies
+
+
+def _wait_all(group, me, n, src_for, land, ssem, rsem, copies):
+    for copy in copies:
+        copy.wait_send()
+    for k in range(1, n):
+        src_rank = lax.rem(me + n - k, n)
+        peer = _peer_coords(group, src_rank)
+        pltpu.make_async_remote_copy(
+            src_ref=src_for(peer), dst_ref=land.at[src_rank], send_sem=ssem.at[k],
+            recv_sem=rsem.at[k], device_id=peer, device_id_type=MESH,
+        ).wait_recv()
+
+
+def _gelu(v):
+    return 0.5 * v * (1.0 + jnp.tanh(0.7978845608028654 * (v + 0.044715 * v * v * v)))
+
+
+def _slots_kernel(n_dp, n_seq, n_ex, num_ref, side_ref, phi_ref, w_in_hbm, w_out_hbm,
+                  phi_out, so_out, w_in_v, w_out_v, w_sem, num_land, side_land, phi_land,
+                  slot_in, part_src, part_land, so_src, so_land, sems):
+    g1, g2 = ("dp", "seq"), ("expert",)
+    n1 = n_dp * n_seq
+    me1, me2 = _my_rank(g1), _my_rank(g2)
+    my_dp = lax.axis_index("dp")
+    w_in_copy = pltpu.make_async_copy(w_in_hbm, w_in_v, w_sem.at[0])
+    w_out_copy = pltpu.make_async_copy(w_out_hbm, w_out_v, w_sem.at[1])
+    w_in_copy.start()
+    w_out_copy.start()
+
+    barrier = pltpu.get_barrier_semaphore()
+    for group, me, n in ((g1, me1, n1), (g2, me2, n_ex)):
+        for k in range(1, n):
+            peer = _peer_coords(group, lax.rem(me + k, n))
+            pl.semaphore_signal(barrier, inc=1, device_id=peer, device_id_type=MESH)
+    pl.semaphore_wait(barrier, n1 - 1 + n_ex - 1)
+
+    stage_a = [
+        (g1, me1, n1, lambda c: num_ref, num_land, sems.at[0], sems.at[1]),
+        (g1, me1, n1, lambda c: side_ref, side_land, sems.at[2], sems.at[3]),
+        (g2, me2, n_ex, lambda c: phi_ref, phi_land, sems.at[4], sems.at[5]),
+    ]
+    started = [_send_all(*args) for args in stage_a]
+    for args, copies in zip(stage_a, started):
+        _wait_all(*args, copies)
+    num_land[me1] = num_ref[...]
+    side_land[me1] = side_ref[...]
+    phi_land[me2] = phi_ref[...]
+    phi_out[...] = phi_land[...]
+
+    own_e = num_ref.shape[0]
+    for c in range(n_dp):
+        rows = pl.ds(c * n_seq, n_seq)
+        side = side_land[rows]
+        part_max = side[:, :, 128:256]
+        scale = jnp.exp(part_max - jnp.max(part_max, axis=0, keepdims=True))
+        denom = jnp.sum(side[:, :, 0:128] * scale, axis=0)
+        numer = jnp.sum(num_land[rows] * scale[:, :, 0:1], axis=0)
+        value = (numer / denom[:, 0:1]).astype(jnp.bfloat16).astype(jnp.float32)
+        for e in range(own_e):
+            slot_in[e, pl.ds(c, 1), :] = value[e:e + 1, :]
+
+    w_in_copy.wait()
+    w_out_copy.wait()
+    for e in range(own_e):
+        hidden = jnp.dot(slot_in[e].astype(jnp.bfloat16), w_in_v[e], preferred_element_type=jnp.float32)
+        hidden = _gelu(hidden).astype(jnp.bfloat16)
+        part = jnp.dot(hidden, w_out_v[e], preferred_element_type=jnp.float32)
+        for c in range(n_dp):
+            part_src[c, pl.ds(e, 1), :] = part[c:c + 1, :]
+
+    dp_pos = AXES.index("dp")
+    stage_b = (g1, me1, n1, lambda c: part_src.at[c[dp_pos]], part_land, sems.at[6], sems.at[7])
+    _wait_all(*stage_b, _send_all(*stage_b))
+    part_land[me1] = part_src[my_dp]
+    so_src[...] = jnp.sum(part_land[...], axis=0).astype(so_src.dtype)
+
+    stage_c = (g2, me2, n_ex, lambda c: so_src, so_land, sems.at[8], sems.at[9])
+    _wait_all(*stage_c, _send_all(*stage_c))
+    so_land[me2] = so_src[...]
+    so_out[...] = so_land[...]
+
+
+def expert_slots(num, side, phi_t, w_in, w_out, cid):
+    n_dp, n_seq, n_ex = (lax.axis_size(a) for a in AXES)
+    n1 = n_dp * n_seq
+    own_e, d = num.shape
+    vmem = pl.BlockSpec(memory_space=pltpu.VMEM)
+    anywhere = pl.BlockSpec(memory_space=pl.ANY)
+    gathered = jax.ShapeDtypeStruct((n_ex, own_e, d), jnp.bfloat16)
+    return pl.pallas_call(
+        functools.partial(_slots_kernel, n_dp, n_seq, n_ex),
+        out_shape=(gathered, gathered),
+        in_specs=[vmem, vmem, vmem, anywhere, anywhere],
+        out_specs=(vmem, vmem),
+        scratch_shapes=[
+            pltpu.VMEM(w_in.shape, w_in.dtype),
+            pltpu.VMEM(w_out.shape, w_out.dtype),
+            pltpu.SemaphoreType.DMA((2,)),
+            pltpu.VMEM((n1, own_e, d), jnp.float32),
+            pltpu.VMEM((n1,) + side.shape, jnp.float32),
+            pltpu.VMEM((n_ex, own_e, d), jnp.bfloat16),
+            pltpu.VMEM((own_e, n_dp, d), jnp.float32),
+            pltpu.VMEM((n_dp, own_e, d), jnp.float32),
+            pltpu.VMEM((n1, own_e, d), jnp.float32),
+            pltpu.VMEM((own_e, d), jnp.bfloat16),
+            pltpu.VMEM((n_ex, own_e, d), jnp.bfloat16),
+            pltpu.SemaphoreType.DMA((10, max(n1, n_ex))),
+        ],
+        compiler_params=pltpu.CompilerParams(
+            collective_id=cid, has_side_effects=True, vmem_limit_bytes=48 * 1024 * 1024
+        ),
+    )(num, side, phi_t, w_in, w_out)
+
 def on_device(tokens, phi, w_in, w_out):
     n_expert = lax.axis_size("expert")
     n_dp = lax.axis_size("dp")
@@ -100,24 +225,16 @@
     logits = lax.dot_general(
         phi, tokens, (((0,), (1,)), ((), ())), preferred_element_type=jnp.float32
     )
-    local_max = jnp.broadcast_to(jnp.max(logits, axis=1)[:, None], (own_e, 128))
-    slot_max = jnp.max(exchange(local_max, ("seq",), 0), axis=0)[:, 0]
-    spread = jnp.exp(logits - slot_max[:, None])
+    local_max = jnp.max(logits, axis=1)
+    spread = jnp.exp(logits - local_max[:, None])
     numerator = jnp.dot(spread.astype(jnp.bfloat16), tokens, preferred_element_type=jnp.float32)
-    denominator = jnp.broadcast_to(jnp.sum(spread, axis=1)[:, None], (own_e, 128))
-    stats = exchange(jnp.concatenate([numerator, denominator], axis=1), ("dp", "seq"), 1)
-    stats = jnp.sum(stats.reshape(n_dp, n_seq, own_e, d + 128), axis=1)
-    slot_in = (stats[:, :, :d] / stats[:, :, d:d + 1]).astype(jnp.bfloat16)
-    hidden = jax.nn.gelu(
-        jnp.einsum("ced,edf->cef", slot_in, w_in, preferred_element_type=jnp.float32),
-        approximate=True,
-    ).astype(jnp.bfloat16)
-    partial_value = jnp.einsum("cef,efd->ced", hidden, w_out, preferred_element_type=jnp.float32)
-    summed = jnp.sum(exchange(partial_value, ("dp", "seq"), 2, select="dp"), axis=0)
-    packed = jnp.concatenate([phi.T, summed.astype(jnp.bfloat16)], axis=0)
-    gathered = exchange(packed, ("expert",), 3)
-    phi_all = gathered[:, :own_e].reshape(n_expert * own_e, d)
-    slot_out = gathered[:, own_e:].reshape(n_expert * own_e, d)
+    denominator = jnp.sum(spread, axis=1)
+    side = jnp.concatenate(
+        [jnp.broadcast_to(denominator[:, None], (own_e, 128)),
+         jnp.broadcast_to(local_max[:, None], (own_e, 128))], axis=1)
+    phi_g, slot_g = expert_slots(numerator, side, phi.T, w_in, w_out, 1)
+    phi_all = phi_g.reshape(n_expert * own_e, d)
+    slot_out = slot_g.reshape(n_expert * own_e, d)
     rows = lax.dynamic_slice_in_dim(tokens, lax.axis_index("expert") * rows_out, rows_out, 0)
     row_logits = lax.dot_general(
         phi_all, rows, (((1,), (1,)), ((), ())), preferred_element_type=jnp.float32

time: 71.9 us -> 43.7 us (0.61)
  Pallas kernels: 50.5 us -> 35.9 us
  matrix products: 13.2 us -> 6.49 us
  other arithmetic: 4.36 us -> 0.24 us
  local copies, waits for them, and re-layouts: 2.97 us -> 0.28 us
    pallas_call x4 -> x1, Pallas kernels: 50.5 us -> 35.9 us  [expert_slots(): pl.pallas_call(functools.partial(_slots_kernel, n_dp, n_seq, n_ex), out_s...]
    dot_general x1 -> x0, matrix products: 4.66 us -> none  [on_device(): jnp.einsum('cef,efd->ced', hidden, w_out, preferred_element_type=jnp.floa...]
    dot_general x1, matrix products: 2.88 us -> 0.7 us  [on_device(): jnp.dot(spread.astype(jnp.bfloat16), tokens, preferred_element_type=jnp.f...]
    reduce_sum x3 -> x1, other arithmetic: 2.28 us -> 0.2 us  [on_device(): denominator = jnp.sum(spread, axis=1)]
    slice x3 -> x0, local copies, waits for them, and re-layouts: 1.49 us -> none  [the longest x1 1.29 us: on_device(): phi_all = gathered[:, :own_e].reshape(n_expert * own_e, d)]
    concatenate x2 -> x1, other arithmetic: 1.25 us -> 0.01 us  [on_device(): jnp.concatenate([jnp.broadcast_to(denominator[:, None], (own_e, 128)), jn...]
where the time goes in v4:
time: 43.7 us; the launch traced here: 43 us
  Pallas kernels  35.9 us (82%)
  matrix products  6.49 us (15%)
    pallas_call x1, Pallas kernels, expert_slots(): pl.pallas_call(functools.partial(_slots_kernel, n_dp, n_seq, n_ex), out_s...  35.9 us
    dot_general x1, matrix products, on_device(): lax.dot_general(phi, tokens, (((0,), (1,)), ((), ())), preferred_element_...  3.65 us
    dot_general x1, matrix products, on_device(): lax.dot_general(phi_all, rows, (((1,), (1,)), ((), ())), preferred_elemen...  1.17 us
    dot_general x1, matrix products, on_device(): lax.dot_general(combine_weights.astype(jnp.bfloat16), slot_out, (((0,), (...  0.97 us

profile of v4, /device:TPU:2, one launch (start us, length us, event | category | flops | bytes accessed | tf_op | source)
XLA Modules:
  0.0 43.0 jit_solution(14756414717087957295)
XLA Ops:
  0.0 0.0 copy-start.2
  0.0 0.0 copy-start
  0.0 0.0 copy-start.1
  0.0 3.7 %fusion.12 = (f32[2]{0:T(128)S(1)}, f32[2,1024]{1,0:T(2,128)S(1)}) fusion(bf16[2048,2]{0,1:T(2,128)(2,1)} %param.5, bf16[1024,2048]{1,0:T(8,128)(2,1)} %param.4), kind=kOutput, calls=%fused_computation.14 | convolution fusion | flops 8390654 | bytes 4210696 | tf_op jit(solution)/shard_map/dot_general | solution.py:225
  3.7 0.2 fusion.7
  3.9 0.1 broadcast_in_dim.4
  3.9 0.1 broadcast_in_dim.5
  4.0 0.0 copy-done.2
  4.0 0.7 %fusion.9.num_ref = f32[2,2048]{1,0:T(2,128)S(1)} fusion(bf16[1024,2048]{1,0:T(8,128)(2,1)S(1)} %copy-done.2, f32[2,1024]{1,0:T(2,128)S(1)} %get-tuple-element.10, f32[2]{0:T(128)S(1)} %get-tuple-element.9), kind=kOutput, calls=%fused_computation.11 | convolution fusion | flops 8392704 | bytes 4218888 | tf_op jit(solution)/shard_map/dot_general | solution.py:230
  4.7 0.0 copy-done
  4.7 0.0 copy-done.1
  4.7 35.9 %shard_map.46 = (bf16[16,2,2048]{2,1,0:T(2,128)(2,1)S(1)}, bf16[16,2,2048]{2,1,0:T(2,128)(2,1)S(1)}) custom-call(f32[2,2048]{1,0:T(2,128)S(1)} %fusion.9.num_ref, f32[2,256]{1,0:T(2,128)S(1)} %pad_maximum_fusion.side_ref, bf16[2,2048]{1,0:T(2,128)(2,1)S(1)} %bitcast.6, bf16[2,2048,512]{2,1,0:T(8,128)(2,1)S(1)} %copy-done, bf16[2,512,2048]{2,1,0:T(8,128)(2,1)} %w_out_hbm.1), custom_call_target="tpu_custom_call" | custom-call | tf_op jit(solution)/shard_map/pallas_call | solution.py:194
  40.7 0.1 reshape.10
  40.7 1.2 %fusion.13 = (f32[64]{0:T(128)S(1)}, f32[32,64]{1,0:T(8,128)S(1)}) fusion(bf16[32,2048]{1,0:T(8,128)(2,1)S(1)} %reshape.10, bf16[1024,2048]{1,0:T(8,128)(2,1)} %param.4, s32[]{:T(128)S(6)} %select_n.3), kind=kOutput, calls=%fused_computation.15 | convolution fusion | flops 8390592 | bytes 401668 | tf_op jit(solution)/shard_map/dot_general | solution.py:239
  41.9 0.1 reshape.11
  42.0 1.0 %fusion = bf16[64,2048]{1,0:T(8,128)(2,1)} fusion(bf16[32,2048]{1,0:T(8,128)(2,1)S(1)} %reshape.11, f32[64]{0:T(128)S(1)} %fusion.3, f32[32,64]{1,0:T(8,128)S(1)} %get-tuple-element.12, f32[64]{0:T(128)S(1)} %get-tuple-element.11), kind=kOutput, calls=%fused_computation.1 | convolution fusion | flops 8654848 | bytes 401920 | tf_op jit(solution)/shard_map/dot_general | solution.py:244
  (2 shorter events, 0.0 us)
Async XLA Ops:
  0.0 4.0 %copy-start.2 = (bf16[1024,2048]{1,0:T(8,128)(2,1)S(1)}, bf16[1024,2048]{1,0:T(8,128)(2,1)}, u32[]{:S(2)}) copy-start(bf16[1024,2048]{1,0:T(8,128)(2,1)} %param.4) | copy-start | bytes 12582916
  0.0 4.7 %copy-start = (bf16[2,2048,512]{2,1,0:T(8,128)(2,1)S(1)}, bf16[2,2048,512]{2,1,0:T(8,128)(2,1)}, u32[]{:S(2)}) copy-start(bf16[2,2048,512]{2,1,0:T(8,128)(2,1)} %w_in_hbm.1) | copy-start | bytes 12582916
  0.0 4.7 %copy-start.1 = (bf16[2048,2]{0,1:T(2,128)(2,1)S(1)}, bf16[2048,2]{0,1:T(2,128)(2,1)}, u32[]{:S(2)}) copy-start(bf16[2048,2]{0,1:T(2,128)(2,1)} %param.5) | copy-start | bytes 24580

commit v5 on v4

--- a/solution.py
+++ b/solution.py
@@ -119,13 +119,15 @@
     return 0.5 * v * (1.0 + jnp.tanh(0.7978845608028654 * (v + 0.044715 * v * v * v)))
 
 
-def _slots_kernel(n_dp, n_seq, n_ex, num_ref, side_ref, phi_ref, w_in_hbm, w_out_hbm,
-                  phi_out, so_out, w_in_v, w_out_v, w_sem, num_land, side_land, phi_land,
-                  slot_in, part_src, part_land, so_src, so_land, sems):
+def _slots_kernel(n_dp, n_seq, n_ex, tok_hbm, phi_ref, w_in_hbm, w_out_hbm,
+                  phi_out, so_out, tok_v, num_ref, side_ref, w_in_v, w_out_v, w_sem, num_land,
+                  side_land, phi_land, slot_in, part_src, part_land, so_src, so_land, sems):
     g1, g2 = ("dp", "seq"), ("expert",)
     n1 = n_dp * n_seq
     me1, me2 = _my_rank(g1), _my_rank(g2)
     my_dp = lax.axis_index("dp")
+    tok_copy = pltpu.make_async_copy(tok_hbm, tok_v, w_sem.at[2])
+    tok_copy.start()
     w_in_copy = pltpu.make_async_copy(w_in_hbm, w_in_v, w_sem.at[0])
     w_out_copy = pltpu.make_async_copy(w_out_hbm, w_out_v, w_sem.at[1])
     w_in_copy.start()
@@ -136,6 +138,17 @@
         for k in range(1, n):
             peer = _peer_coords(group, lax.rem(me + k, n))
             pl.semaphore_signal(barrier, inc=1, device_id=peer, device_id_type=MESH)
+
+    tok_copy.wait()
+    logits = lax.dot_general(
+        phi_ref[...], tok_v[...], (((1,), (1,)), ((), ())), preferred_element_type=jnp.float32
+    )
+    local_max = jnp.max(logits, axis=1, keepdims=True)
+    spread = jnp.exp(logits - local_max)
+    denominator = jnp.sum(spread, axis=1, keepdims=True)
+    num_ref[...] = jnp.dot(spread.astype(jnp.bfloat16), tok_v[...], preferred_element_type=jnp.float32)
+    side_ref[:, 0:128] = jnp.broadcast_to(denominator, (denominator.shape[0], 128))
+    side_ref[:, 128:256] = jnp.broadcast_to(local_max, (local_max.shape[0], 128))
     pl.semaphore_wait(barrier, n1 - 1 + n_ex - 1)
 
     stage_a = [
@@ -184,24 +197,27 @@
     so_out[...] = so_land[...]
 
 
-def expert_slots(num, side, phi_t, w_in, w_out, cid):
+def expert_slots(tokens, phi_t, w_in, w_out, cid):
     n_dp, n_seq, n_ex = (lax.axis_size(a) for a in AXES)
     n1 = n_dp * n_seq
-    own_e, d = num.shape
+    own_e, d = phi_t.shape
     vmem = pl.BlockSpec(memory_space=pltpu.VMEM)
     anywhere = pl.BlockSpec(memory_space=pl.ANY)
     gathered = jax.ShapeDtypeStruct((n_ex, own_e, d), jnp.bfloat16)
     return pl.pallas_call(
         functools.partial(_slots_kernel, n_dp, n_seq, n_ex),
         out_shape=(gathered, gathered),
-        in_specs=[vmem, vmem, vmem, anywhere, anywhere],
+        in_specs=[anywhere, vmem, anywhere, anywhere],
         out_specs=(vmem, vmem),
         scratch_shapes=[
+            pltpu.VMEM(tokens.shape, tokens.dtype),
+            pltpu.VMEM((own_e, d), jnp.float32),
+            pltpu.VMEM((own_e, 256), jnp.float32),
             pltpu.VMEM(w_in.shape, w_in.dtype),
             pltpu.VMEM(w_out.shape, w_out.dtype),
-            pltpu.SemaphoreType.DMA((2,)),
+            pltpu.SemaphoreType.DMA((3,)),
             pltpu.VMEM((n1, own_e, d), jnp.float32),
-            pltpu.VMEM((n1,) + side.shape, jnp.float32),
+            pltpu.VMEM((n1, own_e, 256), jnp.float32),
             pltpu.VMEM((n_ex, own_e, d), jnp.bfloat16),
             pltpu.VMEM((own_e, n_dp, d), jnp.float32),
             pltpu.VMEM((n_dp, own_e, d), jnp.float32),
@@ -213,7 +229,7 @@
         compiler_params=pltpu.CompilerParams(
             collective_id=cid, has_side_effects=True, vmem_limit_bytes=48 * 1024 * 1024
         ),
-    )(num, side, phi_t, w_in, w_out)
+    )(tokens, phi_t, w_in, w_out)
 
 def on_device(tokens, phi, w_in, w_out):
     n_expert = lax.axis_size("expert")
@@ -222,17 +238,7 @@
     own_e = phi.shape[1]
     d = tokens.shape[1]
     rows_out = tokens.shape[0] // n_expert
-    logits = lax.dot_general(
-        phi, tokens, (((0,), (1,)), ((), ())), preferred_element_type=jnp.float32
-    )
-    local_max = jnp.max(logits, axis=1)
-    spread = jnp.exp(logits - local_max[:, None])
-    numerator = jnp.dot(spread.astype(jnp.bfloat16), tokens, preferred_element_type=jnp.float32)
-    denominator = jnp.sum(spread, axis=1)
-    side = jnp.concatenate(
-        [jnp.broadcast_to(denominator[:, None], (own_e, 128)),
-         jnp.broadcast_to(local_max[:, None], (own_e, 128))], axis=1)
-    phi_g, slot_g = expert_slots(numerator, side, phi.T, w_in, w_out, 1)
+    phi_g, slot_g = expert_slots(tokens, phi.T, w_in, w_out, 1)
     phi_all = phi_g.reshape(n_expert * own_e, d)
     slot_out = slot_g.reshape(n_expert * own_e, d)
     rows = lax.dynamic_slice_in_dim(tokens, lax.axis_index("expert") * rows_out, rows_out, 0)

time: 43.7 us -> 41.8 us (0.957)
  matrix products: 6.49 us -> 2.13 us
  local copies, waits for them, and re-layouts: 0.28 us -> 2.99 us
    dot_general x2 -> x0, matrix products: 4.35 us -> none  [the longest x1 3.65 us: on_device(): lax.dot_general(phi, tokens, (((0,), (1,)), ((), ())), preferred_element_...]
    unnamed x6 -> x4, local copies, waits for them, and re-layouts: 0.03 us -> 2.88 us
where the time goes in v5:
time: 41.8 us; the launch traced here: 41.1 us
  Pallas kernels  35.9 us (86%)
  local copies, waits for them, and re-layouts  2.99 us (7%)
  matrix products  2.13 us (5%)
    pallas_call x1, Pallas kernels, expert_slots(): pl.pallas_call(functools.partial(_slots_kernel, n_dp, n_seq, n_ex), out_s...  35.9 us
    unnamed x4, local copies, waits for them, and re-layouts  2.88 us
    dot_general x1, matrix products, on_device(): lax.dot_general(phi_all, rows, (((1,), (1,)), ((), ())), preferred_elemen...  1.17 us
    dot_general x1, matrix products, on_device(): lax.dot_general(combine_weights.astype(jnp.bfloat16), slot_out, (((0,), (...  0.97 us

profile of v5, /device:TPU:2, one launch (start us, length us, event | category | flops | bytes accessed | tf_op | source)
XLA Modules:
  0.0 41.1 jit_solution(1182414368479367579)
XLA Ops:
  0.0 0.0 copy-start
  0.0 2.2 %copy-done = bf16[1024,2048]{1,0:T(8,128)(2,1)S(1)} copy-done((bf16[1024,2048]{1,0:T(8,128)(2,1)S(1)}, bf16[1024,2048]{1,0:T(8,128)(2,1)}, u32[]{:S(2)}) %copy-start) | copy-done | bytes 4194328
  2.2 0.0 copy-start.1
  2.2 0.7 %copy-done.1 = bf16[2048,2]{0,1:T(2,128)(2,1)S(1)} copy-done((bf16[2048,2]{0,1:T(2,128)(2,1)S(1)}, bf16[2048,2]{0,1:T(2,128)(2,1)}, u32[]{:S(2)}) %copy-start.1) | copy-done | bytes 8216
  2.9 35.9 %shard_map.46 = (bf16[16,2,2048]{2,1,0:T(2,128)(2,1)S(1)}, bf16[16,2,2048]{2,1,0:T(2,128)(2,1)S(1)}) custom-call(bf16[1024,2048]{1,0:T(8,128)(2,1)S(1)} %copy-done, bf16[2,2048]{1,0:T(2,128)(2,1)S(1)} %bitcast.3, bf16[2,2048,512]{2,1,0:T(8,128)(2,1)} %w_in_hbm.1, bf16[2,512,2048]{2,1,0:T(8,128)(2,1)} %w_out_hbm.1), custom_call_target="tpu_custom_call" | custom-call | tf_op jit(solution)/shard_map/pallas_call | solution.py:207
  38.8 0.1 reshape.8
  38.8 1.2 %fusion.8 = (f32[64]{0:T(128)S(1)}, f32[32,64]{1,0:T(8,128)S(1)}) fusion(bf16[32,2048]{1,0:T(8,128)(2,1)S(1)} %reshape.8, bf16[1024,2048]{1,0:T(8,128)(2,1)} %tok_hbm.1, s32[]{:T(128)S(6)} %select_n.3), kind=kOutput, calls=%fused_computation.9 | convolution fusion | flops 8390592 | bytes 401668 | tf_op jit(solution)/shard_map/dot_general | solution.py:245
  40.0 0.1 reshape.9
  40.1 1.0 %fusion = bf16[64,2048]{1,0:T(8,128)(2,1)} fusion(bf16[32,2048]{1,0:T(8,128)(2,1)S(1)} %reshape.9, f32[64]{0:T(128)S(1)} %fusion.3, f32[32,64]{1,0:T(8,128)S(1)} %get-tuple-element.10, f32[64]{0:T(128)S(1)} %get-tuple-element.9), kind=kOutput, calls=%fused_computation.1 | convolution fusion | flops 8654848 | bytes 401920 | tf_op jit(solution)/shard_map/dot_general | solution.py:250
  (1 shorter events, 0.0 us)
Async XLA Ops:
  0.0 2.2 %copy-start = (bf16[1024,2048]{1,0:T(8,128)(2,1)S(1)}, bf16[1024,2048]{1,0:T(8,128)(2,1)}, u32[]{:S(2)}) copy-start(bf16[1024,2048]{1,0:T(8,128)(2,1)} %tok_hbm.1) | copy-start | bytes 12582916
  2.2 0.7 %copy-start.1 = (bf16[2048,2]{0,1:T(2,128)(2,1)S(1)}, bf16[2048,2]{0,1:T(2,128)(2,1)}, u32[]{:S(2)}) copy-start(bf16[2048,2]{0,1:T(2,128)(2,1)} %param.5) | copy-start | bytes 24580

commit v6 on v5

--- a/solution.py
+++ b/solution.py
@@ -120,12 +120,11 @@
 
 
 def _slots_kernel(n_dp, n_seq, n_ex, tok_hbm, phi_ref, w_in_hbm, w_out_hbm,
-                  phi_out, so_out, tok_v, num_ref, side_ref, w_in_v, w_out_v, w_sem, num_land,
-                  side_land, phi_land, slot_in, part_src, part_land, so_src, so_land, sems):
-    g1, g2 = ("dp", "seq"), ("expert",)
-    n1 = n_dp * n_seq
-    me1, me2 = _my_rank(g1), _my_rank(g2)
-    my_dp = lax.axis_index("dp")
+                  phi_out, so_out, tok_v, num_ref, side_ref, w_in_v, w_out_v, w_sem,
+                  num_land, side_land, phi_land, si_src, si_land, slot_in, part_src, pp_land,
+                  cs_src, cs_land, so_src, so_land, sems):
+    gs, gp, ge = ("seq",), ("dp",), ("expert",)
+    me_s, me_p, me_e = _my_rank(gs), _my_rank(gp), _my_rank(ge)
     tok_copy = pltpu.make_async_copy(tok_hbm, tok_v, w_sem.at[2])
     tok_copy.start()
     w_in_copy = pltpu.make_async_copy(w_in_hbm, w_in_v, w_sem.at[0])
@@ -134,7 +133,7 @@
     w_out_copy.start()
 
     barrier = pltpu.get_barrier_semaphore()
-    for group, me, n in ((g1, me1, n1), (g2, me2, n_ex)):
+    for group, me, n in ((gs, me_s, n_seq), (gp, me_p, n_dp), (ge, me_e, n_ex)):
         for k in range(1, n):
             peer = _peer_coords(group, lax.rem(me + k, n))
             pl.semaphore_signal(barrier, inc=1, device_id=peer, device_id_type=MESH)
@@ -149,30 +148,32 @@
     num_ref[...] = jnp.dot(spread.astype(jnp.bfloat16), tok_v[...], preferred_element_type=jnp.float32)
     side_ref[:, 0:128] = jnp.broadcast_to(denominator, (denominator.shape[0], 128))
     side_ref[:, 128:256] = jnp.broadcast_to(local_max, (local_max.shape[0], 128))
-    pl.semaphore_wait(barrier, n1 - 1 + n_ex - 1)
+    pl.semaphore_wait(barrier, n_seq - 1 + n_dp - 1 + n_ex - 1)
 
     stage_a = [
-        (g1, me1, n1, lambda c: num_ref, num_land, sems.at[0], sems.at[1]),
-        (g1, me1, n1, lambda c: side_ref, side_land, sems.at[2], sems.at[3]),
-        (g2, me2, n_ex, lambda c: phi_ref, phi_land, sems.at[4], sems.at[5]),
+        (gs, me_s, n_seq, lambda c: num_ref, num_land, sems.at[0], sems.at[1]),
+        (gs, me_s, n_seq, lambda c: side_ref, side_land, sems.at[2], sems.at[3]),
+        (ge, me_e, n_ex, lambda c: phi_ref, phi_land, sems.at[4], sems.at[5]),
     ]
     started = [_send_all(*args) for args in stage_a]
-    for args, copies in zip(stage_a, started):
+    for args, copies in zip(stage_a[:2], started[:2]):
         _wait_all(*args, copies)
-    num_land[me1] = num_ref[...]
-    side_land[me1] = side_ref[...]
-    phi_land[me2] = phi_ref[...]
-    phi_out[...] = phi_land[...]
-
+    num_land[me_s] = num_ref[...]
+    side_land[me_s] = side_ref[...]
+
+    side = side_land[...]
+    part_max = side[:, :, 128:256]
+    scale = jnp.exp(part_max - jnp.max(part_max, axis=0, keepdims=True))
+    denom = jnp.sum(side[:, :, 0:128] * scale, axis=0)
+    numer = jnp.sum(num_land[...] * scale[:, :, 0:1], axis=0)
+    si_src[...] = (numer / denom[:, 0:1]).astype(si_src.dtype)
+
+    stage_a2 = (gp, me_p, n_dp, lambda c: si_src, si_land, sems.at[6], sems.at[7])
+    _wait_all(*stage_a2, _send_all(*stage_a2))
+    si_land[me_p] = si_src[...]
     own_e = num_ref.shape[0]
     for c in range(n_dp):
-        rows = pl.ds(c * n_seq, n_seq)
-        side = side_land[rows]
-        part_max = side[:, :, 128:256]
-        scale = jnp.exp(part_max - jnp.max(part_max, axis=0, keepdims=True))
-        denom = jnp.sum(side[:, :, 0:128] * scale, axis=0)
-        numer = jnp.sum(num_land[rows] * scale[:, :, 0:1], axis=0)
-        value = (numer / denom[:, 0:1]).astype(jnp.bfloat16).astype(jnp.float32)
+        value = si_land[c].astype(jnp.float32)
         for e in range(own_e):
             slot_in[e, pl.ds(c, 1), :] = value[e:e + 1, :]
 
@@ -186,20 +187,27 @@
             part_src[c, pl.ds(e, 1), :] = part[c:c + 1, :]
 
     dp_pos = AXES.index("dp")
-    stage_b = (g1, me1, n1, lambda c: part_src.at[c[dp_pos]], part_land, sems.at[6], sems.at[7])
-    _wait_all(*stage_b, _send_all(*stage_b))
-    part_land[me1] = part_src[my_dp]
-    so_src[...] = jnp.sum(part_land[...], axis=0).astype(so_src.dtype)
-
-    stage_c = (g2, me2, n_ex, lambda c: so_src, so_land, sems.at[8], sems.at[9])
+    stage_b1 = (gp, me_p, n_dp, lambda c: part_src.at[c[dp_pos]], pp_land, sems.at[8], sems.at[9])
+    _wait_all(*stage_b1, _send_all(*stage_b1))
+    partner = lax.rem(me_p + 1, n_dp)
+    cs_src[...] = part_src[me_p] + pp_land[partner]
+
+    stage_b2 = (gs, me_s, n_seq, lambda c: cs_src, cs_land, sems.at[10], sems.at[11])
+    _wait_all(*stage_b2, _send_all(*stage_b2))
+    cs_land[me_s] = cs_src[...]
+    so_src[...] = jnp.sum(cs_land[...], axis=0).astype(so_src.dtype)
+
+    stage_c = (ge, me_e, n_ex, lambda c: so_src, so_land, sems.at[12], sems.at[13])
     _wait_all(*stage_c, _send_all(*stage_c))
-    so_land[me2] = so_src[...]
+    so_land[me_e] = so_src[...]
     so_out[...] = so_land[...]
+    _wait_all(*stage_a[2], started[2])
+    phi_land[me_e] = phi_ref[...]
+    phi_out[...] = phi_land[...]
 
 
 def expert_slots(tokens, phi_t, w_in, w_out, cid):
     n_dp, n_seq, n_ex = (lax.axis_size(a) for a in AXES)
-    n1 = n_dp * n_seq
     own_e, d = phi_t.shape
     vmem = pl.BlockSpec(memory_space=pltpu.VMEM)
     anywhere = pl.BlockSpec(memory_space=pl.ANY)
@@ -216,15 +224,19 @@
             pltpu.VMEM(w_in.shape, w_in.dtype),
             pltpu.VMEM(w_out.shape, w_out.dtype),
             pltpu.SemaphoreType.DMA((3,)),
-            pltpu.VMEM((n1, own_e, d), jnp.float32),
-            pltpu.VMEM((n1, own_e, 256), jnp.float32),
+            pltpu.VMEM((n_seq, own_e, d), jnp.float32),
+            pltpu.VMEM((n_seq, own_e, 256), jnp.float32),
             pltpu.VMEM((n_ex, own_e, d), jnp.bfloat16),
+            pltpu.VMEM((own_e, d), jnp.bfloat16),
+            pltpu.VMEM((n_dp, own_e, d), jnp.bfloat16),
             pltpu.VMEM((own_e, n_dp, d), jnp.float32),
             pltpu.VMEM((n_dp, own_e, d), jnp.float32),
-            pltpu.VMEM((n1, own_e, d), jnp.float32),
+            pltpu.VMEM((n_dp, own_e, d), jnp.float32),
+            pltpu.VMEM((own_e, d), jnp.float32),
+            pltpu.VMEM((n_seq, own_e, d), jnp.float32),
             pltpu.VMEM((own_e, d), jnp.bfloat16),
             pltpu.VMEM((n_ex, own_e, d), jnp.bfloat16),
-            pltpu.SemaphoreType.DMA((10, max(n1, n_ex))),
+            pltpu.SemaphoreType.DMA((14, max(n_dp, n_seq, n_ex))),
         ],
         compiler_params=pltpu.CompilerParams(
             collective_id=cid, has_side_effects=True, vmem_limit_bytes=48 * 1024 * 1024

time: 41.8 us -> 37.9 us (0.907)
  Pallas kernels: 35.9 us -> 32.1 us
    pallas_call x1, Pallas kernels: 35.9 us -> 32.1 us  [expert_slots(): pl.pallas_call(functools.partial(_slots_kernel, n_dp, n_seq, n_ex), out_s...]
where the time goes in v6:
time: 37.9 us; the launch traced here: 37.2 us
  Pallas kernels  32.1 us (85%)
  local copies, waits for them, and re-layouts  2.99 us (8%)
  matrix products  2.13 us (6%)
    pallas_call x1, Pallas kernels, expert_slots(): pl.pallas_call(functools.partial(_slots_kernel, n_dp, n_seq, n_ex), out_s...  32.1 us
    unnamed x4, local copies, waits for them, and re-layouts  2.88 us
    dot_general x1, matrix products, on_device(): lax.dot_general(phi_all, rows, (((1,), (1,)), ((), ())), preferred_elemen...  1.17 us
    dot_general x1, matrix products, on_device(): lax.dot_general(combine_weights.astype(jnp.bfloat16), slot_out, (((0,), (...  0.97 us

profile of v6, /device:TPU:2, one launch (start us, length us, event | category | flops | bytes accessed | tf_op | source)
XLA Modules:
  0.0 37.2 jit_solution(9750058934825442837)
XLA Ops:
  0.0 0.0 copy-start
  0.0 2.2 %copy-done = bf16[1024,2048]{1,0:T(8,128)(2,1)S(1)} copy-done((bf16[1024,2048]{1,0:T(8,128)(2,1)S(1)}, bf16[1024,2048]{1,0:T(8,128)(2,1)}, u32[]{:S(2)}) %copy-start) | copy-done | bytes 4194328
  2.2 0.0 copy-start.1
  2.2 0.7 %copy-done.1 = bf16[2048,2]{0,1:T(2,128)(2,1)S(1)} copy-done((bf16[2048,2]{0,1:T(2,128)(2,1)S(1)}, bf16[2048,2]{0,1:T(2,128)(2,1)}, u32[]{:S(2)}) %copy-start.1) | copy-done | bytes 8216
  2.9 32.1 %shard_map.46 = (bf16[16,2,2048]{2,1,0:T(2,128)(2,1)S(1)}, bf16[16,2,2048]{2,1,0:T(2,128)(2,1)S(1)}) custom-call(bf16[1024,2048]{1,0:T(8,128)(2,1)S(1)} %copy-done, bf16[2,2048]{1,0:T(2,128)(2,1)S(1)} %bitcast.3, bf16[2,2048,512]{2,1,0:T(8,128)(2,1)} %w_in_hbm.1, bf16[2,512,2048]{2,1,0:T(8,128)(2,1)} %w_out_hbm.1), custom_call_target="tpu_custom_call" | custom-call | tf_op jit(solution)/shard_map/pallas_call | solution.py:215
  35.0 0.1 reshape.8
  35.0 1.2 %fusion.8 = (f32[64]{0:T(128)S(1)}, f32[32,64]{1,0:T(8,128)S(1)}) fusion(bf16[32,2048]{1,0:T(8,128)(2,1)S(1)} %reshape.8, bf16[1024,2048]{1,0:T(8,128)(2,1)} %tok_hbm.1, s32[]{:T(128)S(6)} %select_n.3), kind=kOutput, calls=%fused_computation.9 | convolution fusion | flops 8390592 | bytes 401668 | tf_op jit(solution)/shard_map/dot_general | solution.py:257
  36.2 0.1 reshape.9
  36.3 1.0 %fusion = bf16[64,2048]{1,0:T(8,128)(2,1)} fusion(bf16[32,2048]{1,0:T(8,128)(2,1)S(1)} %reshape.9, f32[64]{0:T(128)S(1)} %fusion.3, f32[32,64]{1,0:T(8,128)S(1)} %get-tuple-element.10, f32[64]{0:T(128)S(1)} %get-tuple-element.9), kind=kOutput, calls=%fused_computation.1 | convolution fusion | flops 8654848 | bytes 401920 | tf_op jit(solution)/shard_map/dot_general | solution.py:262
  (1 shorter events, 0.0 us)
Async XLA Ops:
  0.0 2.2 %copy-start = (bf16[1024,2048]{1,0:T(8,128)(2,1)S(1)}, bf16[1024,2048]{1,0:T(8,128)(2,1)}, u32[]{:S(2)}) copy-start(bf16[1024,2048]{1,0:T(8,128)(2,1)} %tok_hbm.1) | copy-start | bytes 12582916
  2.2 0.7 %copy-start.1 = (bf16[2048,2]{0,1:T(2,128)(2,1)S(1)}, bf16[2048,2]{0,1:T(2,128)(2,1)}, u32[]{:S(2)}) copy-start(bf16[2048,2]{0,1:T(2,128)(2,1)} %param.5) | copy-start | bytes 24580

commit v7 on v6

--- a/solution.py
+++ b/solution.py
@@ -120,7 +120,7 @@
 
 
 def _slots_kernel(n_dp, n_seq, n_ex, tok_hbm, phi_ref, w_in_hbm, w_out_hbm,
-                  phi_out, so_out, tok_v, num_ref, side_ref, w_in_v, w_out_v, w_sem,
+                  phi_out, so_out, tok_v, mx_ref, mx_land, num_ref, side_ref, w_in_v, w_out_v, w_sem,
                   num_land, side_land, phi_land, si_src, si_land, slot_in, part_src, pp_land,
                   cs_src, cs_land, so_src, so_land, sems):
     gs, gp, ge = ("seq",), ("dp",), ("expert",)
@@ -142,30 +142,33 @@
     logits = lax.dot_general(
         phi_ref[...], tok_v[...], (((1,), (1,)), ((), ())), preferred_element_type=jnp.float32
     )
-    local_max = jnp.max(logits, axis=1, keepdims=True)
-    spread = jnp.exp(logits - local_max)
+    mx_ref[...] = jnp.broadcast_to(jnp.max(logits, axis=1, keepdims=True), mx_ref.shape)
+    pl.semaphore_wait(barrier, n_seq - 1 + n_dp - 1 + n_ex - 1)
+
+    stage_a0 = (gs, me_s, n_seq, lambda c: mx_ref, mx_land, sems.at[14], sems.at[15])
+    stage_phi = (ge, me_e, n_ex, lambda c: phi_ref, phi_land, sems.at[4], sems.at[5])
+    started_a0 = _send_all(*stage_a0)
+    started_phi = _send_all(*stage_phi)
+    _wait_all(*stage_a0, started_a0)
+    mx_land[me_s] = mx_ref[...]
+    slot_max = jnp.max(mx_land[...], axis=0)[:, 0:1]
+    spread = jnp.exp(logits - slot_max)
     denominator = jnp.sum(spread, axis=1, keepdims=True)
     num_ref[...] = jnp.dot(spread.astype(jnp.bfloat16), tok_v[...], preferred_element_type=jnp.float32)
-    side_ref[:, 0:128] = jnp.broadcast_to(denominator, (denominator.shape[0], 128))
-    side_ref[:, 128:256] = jnp.broadcast_to(local_max, (local_max.shape[0], 128))
-    pl.semaphore_wait(barrier, n_seq - 1 + n_dp - 1 + n_ex - 1)
+    side_ref[...] = jnp.broadcast_to(denominator, side_ref.shape)
 
     stage_a = [
         (gs, me_s, n_seq, lambda c: num_ref, num_land, sems.at[0], sems.at[1]),
         (gs, me_s, n_seq, lambda c: side_ref, side_land, sems.at[2], sems.at[3]),
-        (ge, me_e, n_ex, lambda c: phi_ref, phi_land, sems.at[4], sems.at[5]),
     ]
     started = [_send_all(*args) for args in stage_a]
-    for args, copies in zip(stage_a[:2], started[:2]):
+    for args, copies in zip(stage_a, started):
         _wait_all(*args, copies)
     num_land[me_s] = num_ref[...]
     side_land[me_s] = side_ref[...]
 
-    side = side_land[...]
-    part_max = side[:, :, 128:256]
-    scale = jnp.exp(part_max - jnp.max(part_max, axis=0, keepdims=True))
-    denom = jnp.sum(side[:, :, 0:128] * scale, axis=0)
-    numer = jnp.sum(num_land[...] * scale[:, :, 0:1], axis=0)
+    denom = jnp.sum(side_land[...], axis=0)
+    numer = jnp.sum(num_land[...], axis=0)
     si_src[...] = (numer / denom[:, 0:1]).astype(si_src.dtype)
 
     stage_a2 = (gp, me_p, n_dp, lambda c: si_src, si_land, sems.at[6], sems.at[7])
@@ -201,7 +204,7 @@
     _wait_all(*stage_c, _send_all(*stage_c))
     so_land[me_e] = so_src[...]
     so_out[...] = so_land[...]
-    _wait_all(*stage_a[2], started[2])
+    _wait_all(*stage_phi, started_phi)
     phi_land[me_e] = phi_ref[...]
     phi_out[...] = phi_land[...]
 
@@ -219,13 +222,15 @@
         out_specs=(vmem, vmem),
         scratch_shapes=[
             pltpu.VMEM(tokens.shape, tokens.dtype),
+            pltpu.VMEM((own_e, 128), jnp.float32),
+            pltpu.VMEM((n_seq, own_e, 128), jnp.float32),
             pltpu.VMEM((own_e, d), jnp.float32),
-            pltpu.VMEM((own_e, 256), jnp.float32),
+            pltpu.VMEM((own_e, 128), jnp.float32),
             pltpu.VMEM(w_in.shape, w_in.dtype),
             pltpu.VMEM(w_out.shape, w_out.dtype),
             pltpu.SemaphoreType.DMA((3,)),
             pltpu.VMEM((n_seq, own_e, d), jnp.float32),
-            pltpu.VMEM((n_seq, own_e, 256), jnp.float32),
+            pltpu.VMEM((n_seq, own_e, 128), jnp.float32),
             pltpu.VMEM((n_ex, own_e, d), jnp.bfloat16),
             pltpu.VMEM((own_e, d), jnp.bfloat16),
             pltpu.VMEM((n_dp, own_e, d), jnp.bfloat16),
@@ -236,7 +241,7 @@
             pltpu.VMEM((n_seq, own_e, d), jnp.float32),
             pltpu.VMEM((own_e, d), jnp.bfloat16),
             pltpu.VMEM((n_ex, own_e, d), jnp.bfloat16),
-            pltpu.SemaphoreType.DMA((14, max(n_dp, n_seq, n_ex))),
+            pltpu.SemaphoreType.DMA((16, max(n_dp, n_seq, n_ex))),
         ],
         compiler_params=pltpu.CompilerParams(
             collective_id=cid, has_side_effects=True, vmem_limit_bytes=48 * 1024 * 1024

time: 37.9 us -> 42.8 us (1.13)
  Pallas kernels: 32.1 us -> 37.3 us
    pallas_call x1, Pallas kernels: 32.1 us -> 37.3 us  [expert_slots(): pl.pallas_call(functools.partial(_slots_kernel, n_dp, n_seq, n_ex), out_s...]
where the time goes in v7:
time: 42.8 us; the launch traced here: 42.5 us
  Pallas kernels  37.3 us (87%)
  local copies, waits for them, and re-layouts  2.99 us (7%)
  matrix products  2.13 us (5%)
    pallas_call x1, Pallas kernels, expert_slots(): pl.pallas_call(functools.partial(_slots_kernel, n_dp, n_seq, n_ex), out_s...  37.3 us
    unnamed x4, local copies, waits for them, and re-layouts  2.88 us
    dot_general x1, matrix products, on_device(): lax.dot_general(phi_all, rows, (((1,), (1,)), ((), ())), preferred_elemen...  1.17 us
    dot_general x1, matrix products, on_device(): lax.dot_general(combine_weights.astype(jnp.bfloat16), slot_out, (((0,), (...  0.97 us

profile of v7, /device:TPU:2, one launch (start us, length us, event | category | flops | bytes accessed | tf_op | source)
XLA Modules:
  0.0 42.5 jit_solution(1685409945832338463)
XLA Ops:
  0.0 0.0 copy-start
  0.0 2.2 %copy-done = bf16[1024,2048]{1,0:T(8,128)(2,1)S(1)} copy-done((bf16[1024,2048]{1,0:T(8,128)(2,1)S(1)}, bf16[1024,2048]{1,0:T(8,128)(2,1)}, u32[]{:S(2)}) %copy-start) | copy-done | bytes 4194328
  2.2 0.0 copy-start.1
  2.2 0.7 %copy-done.1 = bf16[2048,2]{0,1:T(2,128)(2,1)S(1)} copy-done((bf16[2048,2]{0,1:T(2,128)(2,1)S(1)}, bf16[2048,2]{0,1:T(2,128)(2,1)}, u32[]{:S(2)}) %copy-start.1) | copy-done | bytes 8216
  2.9 37.3 %shard_map.46 = (bf16[16,2,2048]{2,1,0:T(2,128)(2,1)S(1)}, bf16[16,2,2048]{2,1,0:T(2,128)(2,1)S(1)}) custom-call(bf16[1024,2048]{1,0:T(8,128)(2,1)S(1)} %copy-done, bf16[2,2048]{1,0:T(2,128)(2,1)S(1)} %bitcast.3, bf16[2,2048,512]{2,1,0:T(8,128)(2,1)} %w_in_hbm.1, bf16[2,512,2048]{2,1,0:T(8,128)(2,1)} %w_out_hbm.1), custom_call_target="tpu_custom_call" | custom-call | tf_op jit(solution)/shard_map/pallas_call | solution.py:218
  40.2 0.1 reshape.8
  40.3 1.2 %fusion.8 = (f32[64]{0:T(128)S(1)}, f32[32,64]{1,0:T(8,128)S(1)}) fusion(bf16[32,2048]{1,0:T(8,128)(2,1)S(1)} %reshape.8, bf16[1024,2048]{1,0:T(8,128)(2,1)} %tok_hbm.1, s32[]{:T(128)S(6)} %select_n.3), kind=kOutput, calls=%fused_computation.9 | convolution fusion | flops 8390592 | bytes 401668 | tf_op jit(solution)/shard_map/dot_general | solution.py:262
  41.5 0.1 reshape.9
  41.6 1.0 %fusion = bf16[64,2048]{1,0:T(8,128)(2,1)} fusion(bf16[32,2048]{1,0:T(8,128)(2,1)S(1)} %reshape.9, f32[64]{0:T(128)S(1)} %fusion.3, f32[32,64]{1,0:T(8,128)S(1)} %get-tuple-element.10, f32[64]{0:T(128)S(1)} %get-tuple-element.9), kind=kOutput, calls=%fused_computation.1 | convolution fusion | flops 8654848 | bytes 401920 | tf_op jit(solution)/shard_map/dot_general | solution.py:267
  (1 shorter events, 0.0 us)
Async XLA Ops:
  0.0 2.2 %copy-start = (bf16[1024,2048]{1,0:T(8,128)(2,1)S(1)}, bf16[1024,2048]{1,0:T(8,128)(2,1)}, u32[]{:S(2)}) copy-start(bf16[1024,2048]{1,0:T(8,128)(2,1)} %tok_hbm.1) | copy-start | bytes 12582916
  2.2 0.7 %copy-start.1 = (bf16[2048,2]{0,1:T(2,128)(2,1)S(1)}, bf16[2048,2]{0,1:T(2,128)(2,1)}, u32[]{:S(2)}) copy-start(bf16[2048,2]{0,1:T(2,128)(2,1)} %param.5) | copy-start | bytes 24580

commit v8 on v7

--- a/solution.py
+++ b/solution.py
@@ -120,8 +120,8 @@
 
 
 def _slots_kernel(n_dp, n_seq, n_ex, tok_hbm, phi_ref, w_in_hbm, w_out_hbm,
-                  phi_out, so_out, tok_v, mx_ref, mx_land, num_ref, side_ref, w_in_v, w_out_v, w_sem,
-                  num_land, side_land, phi_land, si_src, si_land, slot_in, part_src, pp_land,
+                  lg_out, so_out, tok_v, mx_ref, mx_land, num_ref, side_ref, w_in_v, w_out_v, w_sem,
+                  num_land, side_land, lg_src, lg_land, si_src, si_land, slot_in, part_src, pp_land,
                   cs_src, cs_land, so_src, so_land, sems):
     gs, gp, ge = ("seq",), ("dp",), ("expert",)
     me_s, me_p, me_e = _my_rank(gs), _my_rank(gp), _my_rank(ge)
@@ -143,10 +143,14 @@
         phi_ref[...], tok_v[...], (((1,), (1,)), ((), ())), preferred_element_type=jnp.float32
     )
     mx_ref[...] = jnp.broadcast_to(jnp.max(logits, axis=1, keepdims=True), mx_ref.shape)
+    rows_out = lg_src.shape[2]
+    for g in range(n_ex):
+        lg_src[g] = logits[:, g * rows_out:(g + 1) * rows_out]
     pl.semaphore_wait(barrier, n_seq - 1 + n_dp - 1 + n_ex - 1)
 
     stage_a0 = (gs, me_s, n_seq, lambda c: mx_ref, mx_land, sems.at[14], sems.at[15])
-    stage_phi = (ge, me_e, n_ex, lambda c: phi_ref, phi_land, sems.at[4], sems.at[5])
+    ex_pos = AXES.index("expert")
+    stage_phi = (ge, me_e, n_ex, lambda c: lg_src.at[c[ex_pos]], lg_land, sems.at[4], sems.at[5])
     started_a0 = _send_all(*stage_a0)
     started_phi = _send_all(*stage_phi)
     _wait_all(*stage_a0, started_a0)
@@ -205,8 +209,8 @@
     so_land[me_e] = so_src[...]
     so_out[...] = so_land[...]
     _wait_all(*stage_phi, started_phi)
-    phi_land[me_e] = phi_ref[...]
-    phi_out[...] = phi_land[...]
+    lg_land[me_e] = lg_src[me_e]
+    lg_out[...] = lg_land[...]
 
 
 def expert_slots(tokens, phi_t, w_in, w_out, cid):
@@ -215,9 +219,11 @@
     vmem = pl.BlockSpec(memory_space=pltpu.VMEM)
     anywhere = pl.BlockSpec(memory_space=pl.ANY)
     gathered = jax.ShapeDtypeStruct((n_ex, own_e, d), jnp.bfloat16)
+    rows_out = tokens.shape[0] // n_ex
+    row_logits = jax.ShapeDtypeStruct((n_ex, own_e, rows_out), jnp.float32)
     return pl.pallas_call(
         functools.partial(_slots_kernel, n_dp, n_seq, n_ex),
-        out_shape=(gathered, gathered),
+        out_shape=(row_logits, gathered),
         in_specs=[anywhere, vmem, anywhere, anywhere],
         out_specs=(vmem, vmem),
         scratch_shapes=[
@@ -231,7 +237,8 @@
             pltpu.SemaphoreType.DMA((3,)),
             pltpu.VMEM((n_seq, own_e, d), jnp.float32),
             pltpu.VMEM((n_seq, own_e, 128), jnp.float32),
-            pltpu.VMEM((n_ex, own_e, d), jnp.bfloat16),
+            pltpu.VMEM((n_ex, own_e, rows_out), jnp.float32),
+            pltpu.VMEM((n_ex, own_e, rows_out), jnp.float32),
             pltpu.VMEM((own_e, d), jnp.bfloat16),
             pltpu.VMEM((n_dp, own_e, d), jnp.bfloat16),
             pltpu.VMEM((own_e, n_dp, d), jnp.float32),
@@ -255,13 +262,9 @@
     own_e = phi.shape[1]
     d = tokens.shape[1]
     rows_out = tokens.shape[0] // n_expert
-    phi_g, slot_g = expert_slots(tokens, phi.T, w_in, w_out, 1)
-    phi_all = phi_g.reshape(n_expert * own_e, d)
+    logit_g, slot_g = expert_slots(tokens, phi.T, w_in, w_out, 1)
+    row_logits = logit_g.reshape(n_expert * own_e, rows_out)
     slot_out = slot_g.reshape(n_expert * own_e, d)
-    rows = lax.dynamic_slice_in_dim(tokens, lax.axis_index("expert") * rows_out, rows_out, 0)
-    row_logits = lax.dot_general(
-        phi_all, rows, (((1,), (1,)), ((), ())), preferred_element_type=jnp.float32
-    )
     row_max = jnp.max(row_logits, axis=0)
     combine_weights = jnp.exp(row_logits - row_max[None, :])
     mixed_numer = lax.dot_general(

time: 42.8 us -> 41.6 us (0.972)
  matrix products: 2.13 us -> 0.96 us
    dot_general x1 -> x0, matrix products: 1.17 us -> none  [on_device(): lax.dot_general(phi_all, rows, (((1,), (1,)), ((), ())), preferred_elemen...]
where the time goes in v8:
time: 41.6 us; the launch traced here: 41.4 us
  Pallas kernels  37.5 us (90%)
  local copies, waits for them, and re-layouts  2.88 us (7%)
  matrix products  0.96 us (2%)
    pallas_call x1, Pallas kernels, expert_slots(): pl.pallas_call(functools.partial(_slots_kernel, n_dp, n_seq, n_ex), out_s...  37.5 us
    unnamed x4, local copies, waits for them, and re-layouts  2.88 us
    dot_general x1, matrix products, on_device(): lax.dot_general(combine_weights.astype(jnp.bfloat16), slot_out, (((0,), (...  0.96 us

profile of v8, /device:TPU:2, one launch (start us, length us, event | category | flops | bytes accessed | tf_op | source)
XLA Modules:
  0.0 41.4 jit_solution(5863542781160306662)
XLA Ops:
  0.0 0.0 copy-start
  0.0 2.2 %copy-done = bf16[1024,2048]{1,0:T(8,128)(2,1)S(1)} copy-done((bf16[1024,2048]{1,0:T(8,128)(2,1)S(1)}, bf16[1024,2048]{1,0:T(8,128)(2,1)}, u32[]{:S(2)}) %copy-start) | copy-done | bytes 4194328
  2.2 0.0 copy-start.1
  2.2 0.7 %copy-done.1 = bf16[2048,2]{0,1:T(2,128)(2,1)S(1)} copy-done((bf16[2048,2]{0,1:T(2,128)(2,1)S(1)}, bf16[2048,2]{0,1:T(2,128)(2,1)}, u32[]{:S(2)}) %copy-start.1) | copy-done | bytes 8216
  2.9 37.5 %shard_map.46 = (f32[16,2,64]{2,1,0:T(2,128)S(1)}, bf16[16,2,2048]{2,1,0:T(2,128)(2,1)S(1)}) custom-call(bf16[1024,2048]{1,0:T(8,128)(2,1)S(1)} %copy-done, bf16[2,2048]{1,0:T(2,128)(2,1)S(1)} %bitcast.7, bf16[2,2048,512]{2,1,0:T(8,128)(2,1)} %w_in_hbm.1, bf16[2,512,2048]{2,1,0:T(8,128)(2,1)} %w_out_hbm.1), custom_call_target="tpu_custom_call" | custom-call | tf_op jit(solution)/shard_map/pallas_call | solution.py:224
  40.5 1.0 %fusion.1 = bf16[64,2048]{1,0:T(8,128)(2,1)} fusion(f32[64]{0:T(128)S(1)} %get-tuple-element.10, bf16[16,2,2048]{2,1,0:T(2,128)(2,1)S(1)} %get-tuple-element.8, bf16[16,2,64]{2,1,0:T(2,128)(2,1)S(1)} %get-tuple-element.9), kind=kOutput, calls=%fused_computation.2 | convolution fusion | flops 8650752 | bytes 397568 | tf_op jit(solution)/shard_map/dot_general | solution.py:270
  (2 shorter events, 0.1 us)
Async XLA Ops:
  0.0 2.2 %copy-start = (bf16[1024,2048]{1,0:T(8,128)(2,1)S(1)}, bf16[1024,2048]{1,0:T(8,128)(2,1)}, u32[]{:S(2)}) copy-start(bf16[1024,2048]{1,0:T(8,128)(2,1)} %tok_hbm.1) | copy-start | bytes 12582916
  2.2 0.7 %copy-start.1 = (bf16[2048,2]{0,1:T(2,128)(2,1)S(1)}, bf16[2048,2]{0,1:T(2,128)(2,1)}, u32[]{:S(2)}) copy-start(bf16[2048,2]{0,1:T(2,128)(2,1)} %param.5) | copy-start | bytes 24580

commit v9 on v8

--- a/solution.py
+++ b/solution.py
@@ -119,14 +119,12 @@
     return 0.5 * v * (1.0 + jnp.tanh(0.7978845608028654 * (v + 0.044715 * v * v * v)))
 
 
-def _slots_kernel(n_dp, n_seq, n_ex, tok_hbm, phi_ref, w_in_hbm, w_out_hbm,
-                  lg_out, so_out, tok_v, mx_ref, mx_land, num_ref, side_ref, w_in_v, w_out_v, w_sem,
+def _slots_kernel(n_dp, n_seq, n_ex, tok_v, phi_ref, w_in_hbm, w_out_hbm,
+                  lg_out, so_out, mx_ref, mx_land, num_ref, side_ref, w_in_v, w_out_v, w_sem,
                   num_land, side_land, lg_src, lg_land, si_src, si_land, slot_in, part_src, pp_land,
                   cs_src, cs_land, so_src, so_land, sems):
     gs, gp, ge = ("seq",), ("dp",), ("expert",)
     me_s, me_p, me_e = _my_rank(gs), _my_rank(gp), _my_rank(ge)
-    tok_copy = pltpu.make_async_copy(tok_hbm, tok_v, w_sem.at[2])
-    tok_copy.start()
     w_in_copy = pltpu.make_async_copy(w_in_hbm, w_in_v, w_sem.at[0])
     w_out_copy = pltpu.make_async_copy(w_out_hbm, w_out_v, w_sem.at[1])
     w_in_copy.start()
@@ -138,7 +136,6 @@
             peer = _peer_coords(group, lax.rem(me + k, n))
             pl.semaphore_signal(barrier, inc=1, device_id=peer, device_id_type=MESH)
 
-    tok_copy.wait()
     logits = lax.dot_general(
         phi_ref[...], tok_v[...], (((1,), (1,)), ((), ())), preferred_element_type=jnp.float32
     )
@@ -224,17 +221,16 @@
     return pl.pallas_call(
         functools.partial(_slots_kernel, n_dp, n_seq, n_ex),
         out_shape=(row_logits, gathered),
-        in_specs=[anywhere, vmem, anywhere, anywhere],
+        in_specs=[vmem, vmem, anywhere, anywhere],
         out_specs=(vmem, vmem),
         scratch_shapes=[
-            pltpu.VMEM(tokens.shape, tokens.dtype),
             pltpu.VMEM((own_e, 128), jnp.float32),
             pltpu.VMEM((n_seq, own_e, 128), jnp.float32),
             pltpu.VMEM((own_e, d), jnp.float32),
             pltpu.VMEM((own_e, 128), jnp.float32),
             pltpu.VMEM(w_in.shape, w_in.dtype),
             pltpu.VMEM(w_out.shape, w_out.dtype),
-            pltpu.SemaphoreType.DMA((3,)),
+            pltpu.SemaphoreType.DMA((2,)),
             pltpu.VMEM((n_seq, own_e, d), jnp.float32),
             pltpu.VMEM((n_seq, own_e, 128), jnp.float32),
             pltpu.VMEM((n_ex, own_e, rows_out), jnp.float32),

time: 41.6 us -> 41 us (0.986)
  Pallas kernels: 37.5 us -> 36.9 us
    pallas_call x1, Pallas kernels: 37.5 us -> 36.9 us  [expert_slots(): pl.pallas_call(functools.partial(_slots_kernel, n_dp, n_seq, n_ex), out_s...]
where the time goes in v9:
time: 41 us; the launch traced here: 40.8 us
  Pallas kernels  36.9 us (90%)
  local copies, waits for them, and re-layouts  2.88 us (7%)
  matrix products  0.96 us (2%)
    pallas_call x1, Pallas kernels, expert_slots(): pl.pallas_call(functools.partial(_slots_kernel, n_dp, n_seq, n_ex), out_s...  36.9 us
    unnamed x4, local copies, waits for them, and re-layouts  2.88 us
    dot_general x1, matrix products, on_device(): lax.dot_general(combine_weights.astype(jnp.bfloat16), slot_out, (((0,), (...  0.96 us

profile of v9, /device:TPU:2, one launch (start us, length us, event | category | flops | bytes accessed | tf_op | source)
XLA Modules:
  0.0 40.8 jit_solution(5354625769994247399)
XLA Ops:
  0.0 0.0 copy-start
  0.0 2.2 %copy-done = bf16[1024,2048]{1,0:T(8,128)(2,1)S(1)} copy-done((bf16[1024,2048]{1,0:T(8,128)(2,1)S(1)}, bf16[1024,2048]{1,0:T(8,128)(2,1)}, u32[]{:S(2)}) %copy-start) | copy-done | bytes 4194328
  2.2 0.0 copy-start.1
  2.2 0.7 %copy-done.1 = bf16[2048,2]{0,1:T(2,128)(2,1)S(1)} copy-done((bf16[2048,2]{0,1:T(2,128)(2,1)S(1)}, bf16[2048,2]{0,1:T(2,128)(2,1)}, u32[]{:S(2)}) %copy-start.1) | copy-done | bytes 8216
  2.9 36.9 %shard_map.46 = (f32[16,2,64]{2,1,0:T(2,128)S(1)}, bf16[16,2,2048]{2,1,0:T(2,128)(2,1)S(1)}) custom-call(bf16[1024,2048]{1,0:T(8,128)(2,1)S(1)} %copy-done, bf16[2,2048]{1,0:T(2,128)(2,1)S(1)} %bitcast.7, bf16[2,2048,512]{2,1,0:T(8,128)(2,1)} %w_in_hbm.1, bf16[2,512,2048]{2,1,0:T(8,128)(2,1)} %w_out_hbm.1), custom_call_target="tpu_custom_call" | custom-call | tf_op jit(solution)/shard_map/pallas_call | solution.py:221
  39.8 1.0 %fusion.1 = bf16[64,2048]{1,0:T(8,128)(2,1)} fusion(f32[64]{0:T(128)S(1)} %get-tuple-element.10, bf16[16,2,2048]{2,1,0:T(2,128)(2,1)S(1)} %get-tuple-element.8, bf16[16,2,64]{2,1,0:T(2,128)(2,1)S(1)} %get-tuple-element.9), kind=kOutput, calls=%fused_computation.2 | convolution fusion | flops 8650752 | bytes 397568 | tf_op jit(solution)/shard_map/dot_general | solution.py:266
  (2 shorter events, 0.1 us)
Async XLA Ops:
  0.0 2.2 %copy-start = (bf16[1024,2048]{1,0:T(8,128)(2,1)S(1)}, bf16[1024,2048]{1,0:T(8,128)(2,1)}, u32[]{:S(2)}) copy-start(bf16[1024,2048]{1,0:T(8,128)(2,1)} %tok_v.1) | copy-start | bytes 12582916
  2.2 0.7 %copy-start.1 = (bf16[2048,2]{0,1:T(2,128)(2,1)S(1)}, bf16[2048,2]{0,1:T(2,128)(2,1)}, u32[]{:S(2)}) copy-start(bf16[2048,2]{0,1:T(2,128)(2,1)} %param.5) | copy-start | bytes 24580

commit v10 on v9

--- a/solution.py
+++ b/solution.py
@@ -120,8 +120,8 @@
 
 
 def _slots_kernel(n_dp, n_seq, n_ex, tok_v, phi_ref, w_in_hbm, w_out_hbm,
-                  lg_out, so_out, mx_ref, mx_land, num_ref, side_ref, w_in_v, w_out_v, w_sem,
-                  num_land, side_land, lg_src, lg_land, si_src, si_land, slot_in, part_src, pp_land,
+                  wb_out, den_out, so_out, mx_ref, mx_land, num_ref, w_in_v, w_out_v, w_sem,
+                  num_land, lg_src, lg_land, si_src, si_land, slot_in, part_src, pp_land,
                   cs_src, cs_land, so_src, so_land, sems):
     gs, gp, ge = ("seq",), ("dp",), ("expert",)
     me_s, me_p, me_e = _my_rank(gs), _my_rank(gp), _my_rank(ge)
@@ -155,22 +155,16 @@
     slot_max = jnp.max(mx_land[...], axis=0)[:, 0:1]
     spread = jnp.exp(logits - slot_max)
     denominator = jnp.sum(spread, axis=1, keepdims=True)
-    num_ref[...] = jnp.dot(spread.astype(jnp.bfloat16), tok_v[...], preferred_element_type=jnp.float32)
-    side_ref[...] = jnp.broadcast_to(denominator, side_ref.shape)
-
-    stage_a = [
-        (gs, me_s, n_seq, lambda c: num_ref, num_land, sems.at[0], sems.at[1]),
-        (gs, me_s, n_seq, lambda c: side_ref, side_land, sems.at[2], sems.at[3]),
-    ]
-    started = [_send_all(*args) for args in stage_a]
-    for args, copies in zip(stage_a, started):
-        _wait_all(*args, copies)
+    d = tok_v.shape[1]
+    num_ref[:, 0:d] = jnp.dot(spread.astype(jnp.bfloat16), tok_v[...], preferred_element_type=jnp.float32)
+    num_ref[:, d:d + 128] = jnp.broadcast_to(denominator, (denominator.shape[0], 128))
+
+    stage_a = (gs, me_s, n_seq, lambda c: num_ref, num_land, sems.at[0], sems.at[1])
+    _wait_all(*stage_a, _send_all(*stage_a))
     num_land[me_s] = num_ref[...]
-    side_land[me_s] = side_ref[...]
-
-    denom = jnp.sum(side_land[...], axis=0)
-    numer = jnp.sum(num_land[...], axis=0)
-    si_src[...] = (numer / denom[:, 0:1]).astype(si_src.dtype)
+
+    totals = jnp.sum(num_land[...], axis=0)
+    si_src[...] = (totals[:, 0:d] / totals[:, d:d + 1]).astype(si_src.dtype)
 
     stage_a2 = (gp, me_p, n_dp, lambda c: si_src, si_land, sems.at[6], sems.at[7])
     _wait_all(*stage_a2, _send_all(*stage_a2))
@@ -202,12 +196,17 @@
     so_src[...] = jnp.sum(cs_land[...], axis=0).astype(so_src.dtype)
 
     stage_c = (ge, me_e, n_ex, lambda c: so_src, so_land, sems.at[12], sems.at[13])
-    _wait_all(*stage_c, _send_all(*stage_c))
+    started_c = _send_all(*stage_c)
+    _wait_all(*stage_phi, started_phi)
+    lg_land[me_e] = lg_src[me_e]
+    row_logits = lg_land[...]
+    row_max = jnp.max(jnp.max(row_logits, axis=0), axis=0, keepdims=True)
+    weights = jnp.exp(row_logits - row_max[None])
+    wb_out[...] = weights.astype(wb_out.dtype)
+    den_out[...] = jnp.sum(jnp.sum(weights, axis=0), axis=0, keepdims=True)
+    _wait_all(*stage_c, started_c)
     so_land[me_e] = so_src[...]
     so_out[...] = so_land[...]
-    _wait_all(*stage_phi, started_phi)
-    lg_land[me_e] = lg_src[me_e]
-    lg_out[...] = lg_land[...]
 
 
 def expert_slots(tokens, phi_t, w_in, w_out, cid):
@@ -217,22 +216,21 @@
     anywhere = pl.BlockSpec(memory_space=pl.ANY)
     gathered = jax.ShapeDtypeStruct((n_ex, own_e, d), jnp.bfloat16)
     rows_out = tokens.shape[0] // n_ex
-    row_logits = jax.ShapeDtypeStruct((n_ex, own_e, rows_out), jnp.float32)
+    weights = jax.ShapeDtypeStruct((n_ex, own_e, rows_out), jnp.bfloat16)
+    totals = jax.ShapeDtypeStruct((1, rows_out), jnp.float32)
     return pl.pallas_call(
         functools.partial(_slots_kernel, n_dp, n_seq, n_ex),
-        out_shape=(row_logits, gathered),
+        out_shape=(weights, totals, gathered),
         in_specs=[vmem, vmem, anywhere, anywhere],
-        out_specs=(vmem, vmem),
+        out_specs=(vmem, vmem, vmem),
         scratch_shapes=[
             pltpu.VMEM((own_e, 128), jnp.float32),
             pltpu.VMEM((n_seq, own_e, 128), jnp.float32),
-            pltpu.VMEM((own_e, d), jnp.float32),
-            pltpu.VMEM((own_e, 128), jnp.float32),
+            pltpu.VMEM((own_e, d + 128), jnp.float32),
             pltpu.VMEM(w_in.shape, w_in.dtype),
             pltpu.VMEM(w_out.shape, w_out.dtype),
             pltpu.SemaphoreType.DMA((2,)),
-            pltpu.VMEM((n_seq, own_e, d), jnp.float32),
-            pltpu.VMEM((n_seq, own_e, 128), jnp.float32),
+            pltpu.VMEM((n_seq, own_e, d + 128), jnp.float32),
             pltpu.VMEM((n_ex, own_e, rows_out), jnp.float32),
             pltpu.VMEM((n_ex, own_e, rows_out), jnp.float32),
             pltpu.VMEM((own_e, d), jnp.bfloat16),
@@ -258,19 +256,16 @@
     own_e = phi.shape[1]
     d = tokens.shape[1]
     rows_out = tokens.shape[0] // n_expert
-    logit_g, slot_g = expert_slots(tokens, phi.T, w_in, w_out, 1)
-    row_logits = logit_g.reshape(n_expert * own_e, rows_out)
+    weight_g, total, slot_g = expert_slots(tokens, phi.T, w_in, w_out, 1)
+    combine_weights = weight_g.reshape(n_expert * own_e, rows_out)
     slot_out = slot_g.reshape(n_expert * own_e, d)
-    row_max = jnp.max(row_logits, axis=0)
-    combine_weights = jnp.exp(row_logits - row_max[None, :])
     mixed_numer = lax.dot_general(
-        combine_weights.astype(jnp.bfloat16),
+        combine_weights,
         slot_out,
         (((0,), (0,)), ((), ())),
         preferred_element_type=jnp.float32,
     )
-    mixed_denom = jnp.sum(combine_weights, axis=0)
-    return (mixed_numer / mixed_denom[:, None]).astype(jnp.bfloat16)
+    return (mixed_numer / total[0][:, None]).astype(jnp.bfloat16)
 
 
 def solution(mesh):

time: 41 us -> 40.6 us (level)
  Pallas kernels: 36.9 us -> 36.3 us
    pallas_call x1, Pallas kernels: 36.9 us -> 36.3 us  [expert_slots(): pl.pallas_call(functools.partial(_slots_kernel, n_dp, n_seq, n_ex), out_s...]
where the time goes in v10:
time: 40.6 us; the launch traced here: 40.2 us
  Pallas kernels  36.3 us (89%)
  local copies, waits for them, and re-layouts  2.88 us (7%)
  matrix products  0.95 us (2%)
    pallas_call x1, Pallas kernels, expert_slots(): pl.pallas_call(functools.partial(_slots_kernel, n_dp, n_seq, n_ex), out_s...  36.3 us
    unnamed x4, local copies, waits for them, and re-layouts  2.88 us
    dot_general x1, matrix products, on_device(): lax.dot_general(combine_weights, slot_out, (((0,), (0,)), ((), ())), pref...  0.95 us

profile of v10, /device:TPU:2, one launch (start us, length us, event | category | flops | bytes accessed | tf_op | source)
XLA Modules:
  0.0 40.2 jit_solution(3946494243552566503)
XLA Ops:
  0.0 0.0 copy-start
  0.0 2.2 %copy-done = bf16[1024,2048]{1,0:T(8,128)(2,1)S(1)} copy-done((bf16[1024,2048]{1,0:T(8,128)(2,1)S(1)}, bf16[1024,2048]{1,0:T(8,128)(2,1)}, u32[]{:S(2)}) %copy-start) | copy-done | bytes 4194328
  2.2 0.0 copy-start.1
  2.2 0.7 %copy-done.1 = bf16[2048,2]{0,1:T(2,128)(2,1)S(1)} copy-done((bf16[2048,2]{0,1:T(2,128)(2,1)S(1)}, bf16[2048,2]{0,1:T(2,128)(2,1)}, u32[]{:S(2)}) %copy-start.1) | copy-done | bytes 8216
  2.9 36.3 %shard_map.46 = (bf16[16,2,64]{2,1,0:T(2,128)(2,1)S(1)}, f32[1,64]{1,0:T(1,128)S(1)}, bf16[16,2,2048]{2,1,0:T(2,128)(2,1)S(1)}) custom-call(bf16[1024,2048]{1,0:T(8,128)(2,1)S(1)} %copy-done, bf16[2,2048]{1,0:T(2,128)(2,1)S(1)} %bitcast.8, bf16[2,2048,512]{2,1,0:T(8,128)(2,1)} %w_in_hbm.1, bf16[2,512,2048]{2,1,0:T(8,128)(2,1)} %w_out_hbm.1), custom_call_target="tpu_custom_call" | custom-call | tf_op jit(solution)/shard_map/pallas_call | solution.py:221
  39.2 1.0 %fusion.1 = bf16[64,2048]{1,0:T(8,128)(2,1)} fusion(f32[64]{0:T(128)S(1)} %bitcast.9, bf16[16,2,2048]{2,1,0:T(2,128)(2,1)S(1)} %get-tuple-element.9, bf16[16,2,64]{2,1,0:T(2,128)(2,1)S(1)} %get-tuple-element.8), kind=kOutput, calls=%fused_computation.2 | convolution fusion | flops 8650752 | bytes 397568 | tf_op jit(solution)/shard_map/dot_general | solution.py:262
Async XLA Ops:
  0.0 2.2 %copy-start = (bf16[1024,2048]{1,0:T(8,128)(2,1)S(1)}, bf16[1024,2048]{1,0:T(8,128)(2,1)}, u32[]{:S(2)}) copy-start(bf16[1024,2048]{1,0:T(8,128)(2,1)} %tok_v.1) | copy-start | bytes 12582916
  2.2 0.7 %copy-start.1 = (bf16[2048,2]{0,1:T(2,128)(2,1)S(1)}, bf16[2048,2]{0,1:T(2,128)(2,1)}, u32[]{:S(2)}) copy-start(bf16[2048,2]{0,1:T(2,128)(2,1)} %param.5) | copy-start | bytes 24580

commit v11 on v10

--- a/solution.py
+++ b/solution.py
@@ -122,7 +122,7 @@
 def _slots_kernel(n_dp, n_seq, n_ex, tok_v, phi_ref, w_in_hbm, w_out_hbm,
                   wb_out, den_out, so_out, mx_ref, mx_land, num_ref, w_in_v, w_out_v, w_sem,
                   num_land, lg_src, lg_land, si_src, si_land, slot_in, part_src, pp_land,
-                  cs_src, cs_land, so_src, so_land, sems):
+                  cs_src, cs_land, so_src, so_land, sems, b1_sems, b2_sems):
     gs, gp, ge = ("seq",), ("dp",), ("expert",)
     me_s, me_p, me_e = _my_rank(gs), _my_rank(gp), _my_rank(ge)
     w_in_copy = pltpu.make_async_copy(w_in_hbm, w_in_v, w_sem.at[0])
@@ -177,23 +177,45 @@
 
     w_in_copy.wait()
     w_out_copy.wait()
+    partner = lax.rem(me_p + 1, n_dp)
+    partner_dev = _peer_coords(gp, partner)
+    seq_peers = [_peer_coords(gs, lax.rem(me_s + j, n_seq)) for j in range(1, n_seq)]
+    seq_srcs = [lax.rem(me_s + n_seq - j, n_seq) for j in range(1, n_seq)]
+    b1 = []
     for e in range(own_e):
         hidden = jnp.dot(slot_in[e].astype(jnp.bfloat16), w_in_v[e], preferred_element_type=jnp.float32)
         hidden = _gelu(hidden).astype(jnp.bfloat16)
-        part = jnp.dot(hidden, w_out_v[e], preferred_element_type=jnp.float32)
-        for c in range(n_dp):
-            part_src[c, pl.ds(e, 1), :] = part[c:c + 1, :]
-
-    dp_pos = AXES.index("dp")
-    stage_b1 = (gp, me_p, n_dp, lambda c: part_src.at[c[dp_pos]], pp_land, sems.at[8], sems.at[9])
-    _wait_all(*stage_b1, _send_all(*stage_b1))
-    partner = lax.rem(me_p + 1, n_dp)
-    cs_src[...] = part_src[me_p] + pp_land[partner]
-
-    stage_b2 = (gs, me_s, n_seq, lambda c: cs_src, cs_land, sems.at[10], sems.at[11])
-    _wait_all(*stage_b2, _send_all(*stage_b2))
+        part_src[e] = jnp.dot(hidden, w_out_v[e], preferred_element_type=jnp.float32)
+        copy = pltpu.make_async_remote_copy(
+            src_ref=part_src.at[e], dst_ref=pp_land.at[e], send_sem=b1_sems.at[e, 0],
+            recv_sem=b1_sems.at[e, 1], device_id=partner_dev, device_id_type=MESH,
+        )
+        copy.start()
+        b1.append(copy)
+    b2 = []
+    for e in range(own_e):
+        b1[e].wait_send()
+        b1[e].wait_recv()
+        cs_src[e] = part_src[e, pl.ds(me_p, 1), :] + pp_land[e, pl.ds(me_p, 1), :]
+        for j in range(1, n_seq):
+            copy = pltpu.make_async_remote_copy(
+                src_ref=cs_src.at[e], dst_ref=cs_land.at[me_s, e], send_sem=b2_sems.at[e, 0, j],
+                recv_sem=b2_sems.at[e, 1, j], device_id=seq_peers[j - 1], device_id_type=MESH,
+            )
+            copy.start()
+            b2.append(copy)
+    for copy in b2:
+        copy.wait_send()
+    for e in range(own_e):
+        for j in range(1, n_seq):
+            pltpu.make_async_remote_copy(
+                src_ref=cs_src.at[e], dst_ref=cs_land.at[seq_srcs[j - 1], e],
+                send_sem=b2_sems.at[e, 0, j], recv_sem=b2_sems.at[e, 1, j],
+                device_id=_peer_coords(gs, seq_srcs[j - 1]), device_id_type=MESH,
+            ).wait_recv()
     cs_land[me_s] = cs_src[...]
-    so_src[...] = jnp.sum(cs_land[...], axis=0).astype(so_src.dtype)
+    total = jnp.sum(cs_land[...], axis=0)
+    so_src[...] = jnp.concatenate([total[e] for e in range(own_e)], axis=0).astype(so_src.dtype)
 
     stage_c = (ge, me_e, n_ex, lambda c: so_src, so_land, sems.at[12], sems.at[13])
     started_c = _send_all(*stage_c)
@@ -236,13 +258,15 @@
             pltpu.VMEM((own_e, d), jnp.bfloat16),
             pltpu.VMEM((n_dp, own_e, d), jnp.bfloat16),
             pltpu.VMEM((own_e, n_dp, d), jnp.float32),
-            pltpu.VMEM((n_dp, own_e, d), jnp.float32),
-            pltpu.VMEM((n_dp, own_e, d), jnp.float32),
-            pltpu.VMEM((own_e, d), jnp.float32),
-            pltpu.VMEM((n_seq, own_e, d), jnp.float32),
+            pltpu.VMEM((own_e, n_dp, d), jnp.float32),
+            pltpu.VMEM((own_e, n_dp, d), jnp.float32),
+            pltpu.VMEM((own_e, 1, d), jnp.float32),
+            pltpu.VMEM((n_seq, own_e, 1, d), jnp.float32),
             pltpu.VMEM((own_e, d), jnp.bfloat16),
             pltpu.VMEM((n_ex, own_e, d), jnp.bfloat16),
             pltpu.SemaphoreType.DMA((16, max(n_dp, n_seq, n_ex))),
+            pltpu.SemaphoreType.DMA((own_e, 2)),
+            pltpu.SemaphoreType.DMA((own_e, 2, n_seq)),
         ],
         compiler_params=pltpu.CompilerParams(
             collective_id=cid, has_side_effects=True, vmem_limit_bytes=48 * 1024 * 1024

time: 40.6 us -> 40.4 us (level)
  no operation moved by 1% of the time
where the time goes in v11:
time: 40.4 us; the launch traced here: 40.1 us
  Pallas kernels  36.3 us (90%)
  local copies, waits for them, and re-layouts  2.88 us (7%)
  matrix products  0.95 us (2%)
    pallas_call x1, Pallas kernels, expert_slots(): pl.pallas_call(functools.partial(_slots_kernel, n_dp, n_seq, n_ex), out_s...  36.3 us
    unnamed x4, local copies, waits for them, and re-layouts  2.88 us
    dot_general x1, matrix products, on_device(): lax.dot_general(combine_weights, slot_out, (((0,), (0,)), ((), ())), pref...  0.95 us

profile of v11, /device:TPU:2, one launch (start us, length us, event | category | flops | bytes accessed | tf_op | source)
XLA Modules:
  0.0 40.1 jit_solution(3465629636314407352)
XLA Ops:
  0.0 0.0 copy-start
  0.0 2.2 %copy-done = bf16[1024,2048]{1,0:T(8,128)(2,1)S(1)} copy-done((bf16[1024,2048]{1,0:T(8,128)(2,1)S(1)}, bf16[1024,2048]{1,0:T(8,128)(2,1)}, u32[]{:S(2)}) %copy-start) | copy-done | bytes 4194328
  2.2 0.0 copy-start.1
  2.2 0.7 %copy-done.1 = bf16[2048,2]{0,1:T(2,128)(2,1)S(1)} copy-done((bf16[2048,2]{0,1:T(2,128)(2,1)S(1)}, bf16[2048,2]{0,1:T(2,128)(2,1)}, u32[]{:S(2)}) %copy-start.1) | copy-done | bytes 8216
  2.9 36.3 %shard_map.46 = (bf16[16,2,64]{2,1,0:T(2,128)(2,1)S(1)}, f32[1,64]{1,0:T(1,128)S(1)}, bf16[16,2,2048]{2,1,0:T(2,128)(2,1)S(1)}) custom-call(bf16[1024,2048]{1,0:T(8,128)(2,1)S(1)} %copy-done, bf16[2,2048]{1,0:T(2,128)(2,1)S(1)} %bitcast.8, bf16[2,2048,512]{2,1,0:T(8,128)(2,1)} %w_in_hbm.1, bf16[2,512,2048]{2,1,0:T(8,128)(2,1)} %w_out_hbm.1), custom_call_target="tpu_custom_call" | custom-call | tf_op jit(solution)/shard_map/pallas_call | solution.py:243
  39.2 1.0 %fusion.1 = bf16[64,2048]{1,0:T(8,128)(2,1)} fusion(f32[64]{0:T(128)S(1)} %bitcast.9, bf16[16,2,2048]{2,1,0:T(2,128)(2,1)S(1)} %get-tuple-element.9, bf16[16,2,64]{2,1,0:T(2,128)(2,1)S(1)} %get-tuple-element.8), kind=kOutput, calls=%fused_computation.2 | convolution fusion | flops 8650752 | bytes 397568 | tf_op jit(solution)/shard_map/dot_general | solution.py:286
Async XLA Ops:
  0.0 2.2 %copy-start = (bf16[1024,2048]{1,0:T(8,128)(2,1)S(1)}, bf16[1024,2048]{1,0:T(8,128)(2,1)}, u32[]{:S(2)}) copy-start(bf16[1024,2048]{1,0:T(8,128)(2,1)} %tok_v.1) | copy-start | bytes 12582916
  2.2 0.7 %copy-start.1 = (bf16[2048,2]{0,1:T(2,128)(2,1)S(1)}, bf16[2048,2]{0,1:T(2,128)(2,1)}, u32[]{:S(2)}) copy-start(bf16[2048,2]{0,1:T(2,128)(2,1)} %param.5) | copy-start | bytes 24580

commit v12 on v10

--- a/solution.py
+++ b/solution.py
@@ -90,9 +90,15 @@
     )(x)
 
 
+def _issue_order(group, n):
+    if group == ("seq",):
+        return sorted(range(1, n), key=lambda k: -min(k, n - k))
+    return list(range(1, n))
+
+
 def _send_all(group, me, n, src_for, land, ssem, rsem):
     copies = []
-    for k in range(1, n):
+    for k in _issue_order(group, n):
         peer = _peer_coords(group, lax.rem(me + k, n))
         copy = pltpu.make_async_remote_copy(
             src_ref=src_for(peer), dst_ref=land.at[me], send_sem=ssem.at[k],
@@ -132,7 +138,7 @@
 
     barrier = pltpu.get_barrier_semaphore()
     for group, me, n in ((gs, me_s, n_seq), (gp, me_p, n_dp), (ge, me_e, n_ex)):
-        for k in range(1, n):
+        for k in _issue_order(group, n):
             peer = _peer_coords(group, lax.rem(me + k, n))
             pl.semaphore_signal(barrier, inc=1, device_id=peer, device_id_type=MESH)
 

time: 40.6 us -> 39.4 us (0.970)
  Pallas kernels: 36.3 us -> 34.8 us
    pallas_call x1, Pallas kernels: 36.3 us -> 34.8 us  [expert_slots(): pl.pallas_call(functools.partial(_slots_kernel, n_dp, n_seq, n_ex), out_s...]
where the time goes in v12:
time: 39.4 us; the launch traced here: 38.6 us
  Pallas kernels  34.8 us (88%)
  local copies, waits for them, and re-layouts  2.88 us (7%)
  matrix products  0.96 us (2%)
    pallas_call x1, Pallas kernels, expert_slots(): pl.pallas_call(functools.partial(_slots_kernel, n_dp, n_seq, n_ex), out_s...  34.8 us
    unnamed x4, local copies, waits for them, and re-layouts  2.88 us
    dot_general x1, matrix products, on_device(): lax.dot_general(combine_weights, slot_out, (((0,), (0,)), ((), ())), pref...  0.96 us

profile of v12, /device:TPU:2, one launch (start us, length us, event | category | flops | bytes accessed | tf_op | source)
XLA Modules:
  0.0 38.6 jit_solution(4776181546306683350)
XLA Ops:
  0.0 0.0 copy-start
  0.0 2.2 %copy-done = bf16[1024,2048]{1,0:T(8,128)(2,1)S(1)} copy-done((bf16[1024,2048]{1,0:T(8,128)(2,1)S(1)}, bf16[1024,2048]{1,0:T(8,128)(2,1)}, u32[]{:S(2)}) %copy-start) | copy-done | bytes 4194328
  2.2 0.0 copy-start.1
  2.2 0.7 %copy-done.1 = bf16[2048,2]{0,1:T(2,128)(2,1)S(1)} copy-done((bf16[2048,2]{0,1:T(2,128)(2,1)S(1)}, bf16[2048,2]{0,1:T(2,128)(2,1)}, u32[]{:S(2)}) %copy-start.1) | copy-done | bytes 8216
  2.9 34.8 %shard_map.46 = (bf16[16,2,64]{2,1,0:T(2,128)(2,1)S(1)}, f32[1,64]{1,0:T(1,128)S(1)}, bf16[16,2,2048]{2,1,0:T(2,128)(2,1)S(1)}) custom-call(bf16[1024,2048]{1,0:T(8,128)(2,1)S(1)} %copy-done, bf16[2,2048]{1,0:T(2,128)(2,1)S(1)} %bitcast.8, bf16[2,2048,512]{2,1,0:T(8,128)(2,1)} %w_in_hbm.1, bf16[2,512,2048]{2,1,0:T(8,128)(2,1)} %w_out_hbm.1), custom_call_target="tpu_custom_call" | custom-call | tf_op jit(solution)/shard_map/pallas_call | solution.py:227
  37.7 1.0 %fusion.1 = bf16[64,2048]{1,0:T(8,128)(2,1)} fusion(f32[64]{0:T(128)S(1)} %bitcast.9, bf16[16,2,2048]{2,1,0:T(2,128)(2,1)S(1)} %get-tuple-element.9, bf16[16,2,64]{2,1,0:T(2,128)(2,1)S(1)} %get-tuple-element.8), kind=kOutput, calls=%fused_computation.2 | convolution fusion | flops 8650752 | bytes 397568 | tf_op jit(solution)/shard_map/dot_general | solution.py:268
Async XLA Ops:
  0.0 2.2 %copy-start = (bf16[1024,2048]{1,0:T(8,128)(2,1)S(1)}, bf16[1024,2048]{1,0:T(8,128)(2,1)}, u32[]{:S(2)}) copy-start(bf16[1024,2048]{1,0:T(8,128)(2,1)} %tok_v.1) | copy-start | bytes 12582916
  2.2 0.7 %copy-start.1 = (bf16[2048,2]{0,1:T(2,128)(2,1)S(1)}, bf16[2048,2]{0,1:T(2,128)(2,1)}, u32[]{:S(2)}) copy-start(bf16[2048,2]{0,1:T(2,128)(2,1)} %param.5) | copy-start | bytes 24580

commit v13 on v12

--- a/solution.py
+++ b/solution.py
@@ -90,16 +90,36 @@
     )(x)
 
 
+def _grid(group, n):
+    side = int(round(n ** 0.5))
+    if group == ("expert",) and side * side == n:
+        return side
+    return None
+
+
 def _issue_order(group, n):
-    if group == ("seq",):
-        return sorted(range(1, n), key=lambda k: -min(k, n - k))
-    return list(range(1, n))
+    side = _grid(group, n)
+    if side is None:
+        if group == ("seq",):
+            return sorted(range(1, n), key=lambda k: -min(k, n - k))
+        return list(range(1, n))
+    ring = lambda v: min(v, side - v)
+    return sorted(range(1, n), key=lambda k: -(ring(k // side) + ring(k % side)))
+
+
+def _offset_rank(group, n, me, k, sign):
+    side = _grid(group, n)
+    if side is None:
+        return lax.rem(me + sign * k + n, n)
+    row = lax.rem(me // side + sign * (k // side) + side, side)
+    col = lax.rem(lax.rem(me, side) + sign * (k % side) + side, side)
+    return row * side + col
 
 
 def _send_all(group, me, n, src_for, land, ssem, rsem):
     copies = []
     for k in _issue_order(group, n):
-        peer = _peer_coords(group, lax.rem(me + k, n))
+        peer = _peer_coords(group, _offset_rank(group, n, me, k, 1))
         copy = pltpu.make_async_remote_copy(
             src_ref=src_for(peer), dst_ref=land.at[me], send_sem=ssem.at[k],
             recv_sem=rsem.at[k], device_id=peer, device_id_type=MESH,
@@ -113,7 +133,7 @@
     for copy in copies:
         copy.wait_send()
     for k in range(1, n):
-        src_rank = lax.rem(me + n - k, n)
+        src_rank = _offset_rank(group, n, me, k, -1)
         peer = _peer_coords(group, src_rank)
         pltpu.make_async_remote_copy(
             src_ref=src_for(peer), dst_ref=land.at[src_rank], send_sem=ssem.at[k],
@@ -139,7 +159,7 @@
     barrier = pltpu.get_barrier_semaphore()
     for group, me, n in ((gs, me_s, n_seq), (gp, me_p, n_dp), (ge, me_e, n_ex)):
         for k in _issue_order(group, n):
-            peer = _peer_coords(group, lax.rem(me + k, n))
+            peer = _peer_coords(group, _offset_rank(group, n, me, k, 1))
             pl.semaphore_signal(barrier, inc=1, device_id=peer, device_id_type=MESH)
 
     logits = lax.dot_general(

time: 39.4 us -> 39.2 us (level)
  no operation moved by 1% of the time
where the time goes in v13:
time: 39.2 us; the launch traced here: 38.6 us
  Pallas kernels  34.7 us (89%)
  local copies, waits for them, and re-layouts  2.88 us (7%)
  matrix products  0.96 us (2%)
    pallas_call x1, Pallas kernels, expert_slots(): pl.pallas_call(functools.partial(_slots_kernel, n_dp, n_seq, n_ex), out_s...  34.7 us
    unnamed x4, local copies, waits for them, and re-layouts  2.88 us
    dot_general x1, matrix products, on_device(): lax.dot_general(combine_weights, slot_out, (((0,), (0,)), ((), ())), pref...  0.96 us

profile of v13, /device:TPU:2, one launch (start us, length us, event | category | flops | bytes accessed | tf_op | source)
XLA Modules:
  0.0 38.6 jit_solution(12398105111523485976)
XLA Ops:
  0.0 0.0 copy-start
  0.0 2.2 %copy-done = bf16[1024,2048]{1,0:T(8,128)(2,1)S(1)} copy-done((bf16[1024,2048]{1,0:T(8,128)(2,1)S(1)}, bf16[1024,2048]{1,0:T(8,128)(2,1)}, u32[]{:S(2)}) %copy-start) | copy-done | bytes 4194328
  2.2 0.0 copy-start.1
  2.2 0.7 %copy-done.1 = bf16[2048,2]{0,1:T(2,128)(2,1)S(1)} copy-done((bf16[2048,2]{0,1:T(2,128)(2,1)S(1)}, bf16[2048,2]{0,1:T(2,128)(2,1)}, u32[]{:S(2)}) %copy-start.1) | copy-done | bytes 8216
  2.9 34.7 %shard_map.46 = (bf16[16,2,64]{2,1,0:T(2,128)(2,1)S(1)}, f32[1,64]{1,0:T(1,128)S(1)}, bf16[16,2,2048]{2,1,0:T(2,128)(2,1)S(1)}) custom-call(bf16[1024,2048]{1,0:T(8,128)(2,1)S(1)} %copy-done, bf16[2,2048]{1,0:T(2,128)(2,1)S(1)} %bitcast.8, bf16[2,2048,512]{2,1,0:T(8,128)(2,1)} %w_in_hbm.1, bf16[2,512,2048]{2,1,0:T(8,128)(2,1)} %w_out_hbm.1), custom_call_target="tpu_custom_call" | custom-call | tf_op jit(solution)/shard_map/pallas_call | solution.py:247
  37.6 1.0 %fusion.1 = bf16[64,2048]{1,0:T(8,128)(2,1)} fusion(f32[64]{0:T(128)S(1)} %bitcast.9, bf16[16,2,2048]{2,1,0:T(2,128)(2,1)S(1)} %get-tuple-element.9, bf16[16,2,64]{2,1,0:T(2,128)(2,1)S(1)} %get-tuple-element.8), kind=kOutput, calls=%fused_computation.2 | convolution fusion | flops 8650752 | bytes 397568 | tf_op jit(solution)/shard_map/dot_general | solution.py:288
Async XLA Ops:
  0.0 2.2 %copy-start = (bf16[1024,2048]{1,0:T(8,128)(2,1)S(1)}, bf16[1024,2048]{1,0:T(8,128)(2,1)}, u32[]{:S(2)}) copy-start(bf16[1024,2048]{1,0:T(8,128)(2,1)} %tok_v.1) | copy-start | bytes 12582916
  2.2 0.7 %copy-start.1 = (bf16[2048,2]{0,1:T(2,128)(2,1)S(1)}, bf16[2048,2]{0,1:T(2,128)(2,1)}, u32[]{:S(2)}) copy-start(bf16[2048,2]{0,1:T(2,128)(2,1)} %param.5) | copy-start | bytes 24580
